TPU v7x, 256 devices: a whole 4x4x8 slice. The times are simulated.
256 devices in a mesh: inst: 16 (over x, y), page: 8 (over z), head: 2 (over core).
Axes of the slice: x: 4, y: 4, z: 8, core: 2. Of those that a mesh axis runs over, the one named last changes fastest.
Arguments:
- queries: bfloat16 [32, 8192], P('inst', 'head'), may hold values from -21 to 21
- fresh_key_value: bfloat16 [2, 32, 1024], P(None, 'inst', 'head'), may hold values from -8 to 8
- key_value_pool: bfloat16 [2, 16384, 16, 1024], P(None, ('inst', 'page'), None, 'head'), may hold values from -21 to 21
- block_table: int32 [32, 768], P('inst'), may hold values from -1 to 16383, as said below
- lengths: int32 [32], P('inst'), may hold values from 17 to 12288, as said below
Outputs:
- attn: bfloat16 [32, 8192], P('inst', 'head')
Inputs may be any that keep to these rules, and one draw needn't show every extreme that they name: `block_table`: request r is owned by instance r // 2. Entries 0 to ceil(lengths[r] / 16) - 1 of row r are pool page numbers below 16384, distinct over all requests; every other entry is -1. `lengths`: every request has two or more pages; some request has exactly 768 full pages.
All inputs are finite; a program needn't handle non-finite values.
Results may differ from a plain program's by a relative error of at most 0.001.
Values may be sent and summed in bfloat16 or wider, within the bound.
No kernel may reach another device: no remote copies, remote signals or barrier semaphores. Data moves between devices by JAX's collectives and lax.ppermute only.
A program may use at most 192 MiB of HBM per device.

v0:
```python
import math

import jax
import jax.numpy as jnp
from jax import lax
from jax.sharding import PartitionSpec as P

HEAD_SIZE = 128


LOWEST_SCORE = -1e30


def slot_owners(all_tables, all_lengths, slots, page_tok):
    requests, most_pages = all_tables.shape
    first_page = (lax.axis_index("inst") * lax.axis_size("page") + lax.axis_index("page")) * slots
    column = jnp.arange(most_pages, dtype=jnp.int32)
    live_page = column[None, :] * page_tok < all_lengths[:, None]
    local_page = all_tables - first_page
    inside = live_page & (local_page >= 0) & (local_page < slots)
    expected_output = jnp.where(inside, local_page, slots).reshape(-1)
    request_ids = jnp.broadcast_to(
        jnp.arange(requests, dtype=jnp.int32)[:, None], (requests, most_pages)
    ).reshape(-1)
    page_fill = jnp.clip(all_lengths[:, None] - column[None, :] * page_tok, 0, page_tok).reshape(-1)
    page_owner = (
        jnp.full((slots,), requests, jnp.int32).at[expected_output].set(request_ids, mode="drop")
    )
    filled = jnp.zeros((slots,), jnp.int32).at[expected_output].set(page_fill, mode="drop")
    return (page_owner, filled)


def page_partials(slot_queries, key_value_pool, filled):
    slots = key_value_pool.shape[1]
    page_tok = key_value_pool.shape[2]
    groups = key_value_pool.shape[3] // HEAD_SIZE
    heads = slot_queries.shape[1] // HEAD_SIZE
    grouped_queries = slot_queries.reshape(slots, groups, heads // groups, HEAD_SIZE)
    paged_keys = key_value_pool[0].reshape(slots, page_tok, groups, HEAD_SIZE)
    paged_values = key_value_pool[1].reshape(slots, page_tok, groups, HEAD_SIZE)
    scores = jnp.einsum(
        "sgqd,stgd->sgqt", grouped_queries, paged_keys, preferred_element_type=jnp.float32
    ) * (1.0 / math.sqrt(HEAD_SIZE))
    offsets = jnp.arange(page_tok, dtype=jnp.int32)
    valid = (offsets[None, :] < filled[:, None])[:, None, None, :]
    masked = jnp.where(valid, scores, LOWEST_SCORE)
    page_max = jnp.max(masked, axis=3)
    raw_weight = jnp.where(valid, jnp.exp(masked - page_max[..., None]), 0.0)
    page_sum = jnp.sum(raw_weight, axis=3)
    page_out = jnp.einsum(
        "sgqt,stgd->sgqd",
        raw_weight.astype(jnp.bfloat16),
        paged_values,
        preferred_element_type=jnp.float32,
    )
    return (
        page_max.reshape(slots, heads),
        page_sum.reshape(slots, heads),
        page_out.reshape(slots, heads * HEAD_SIZE),
    )


def request_max(page_max, page_owner, requests):
    matches = page_owner[None, :] == jnp.arange(requests, dtype=jnp.int32)[:, None]
    return jnp.max(jnp.where(matches[:, :, None], page_max[None], LOWEST_SCORE), axis=1)


def request_sums(page_max, page_sum, page_out, page_owner, shared_max):
    requests, heads = shared_max.shape
    slots = page_max.shape[0]
    padded = jnp.concatenate([shared_max, jnp.full((1, heads), LOWEST_SCORE, jnp.float32)], axis=0)
    factor = jnp.exp(page_max - padded[page_owner])
    one_hot = (page_owner[None, :] == jnp.arange(requests, dtype=jnp.int32)[:, None]).astype(
        jnp.float32
    )
    scaled_out = (page_out.reshape(slots, heads, HEAD_SIZE) * factor[:, :, None]).reshape(
        slots, heads * HEAD_SIZE
    )
    summed_out = jnp.dot(
        one_hot, scaled_out, precision=lax.Precision.HIGHEST, preferred_element_type=jnp.float32
    )
    summed_total = jnp.dot(
        one_hot,
        page_sum * factor,
        precision=lax.Precision.HIGHEST,
        preferred_element_type=jnp.float32,
    )
    return (summed_total, summed_out)


def finish(queries, fresh_key_value, cache_max, cache_total, cache_out):
    own_rows = queries.shape[0]
    heads = queries.shape[1] // HEAD_SIZE
    groups = fresh_key_value.shape[2] // HEAD_SIZE
    per_group = heads // groups
    grouped_queries = queries.reshape(own_rows, groups, per_group, HEAD_SIZE)
    new_keys = fresh_key_value[0].reshape(own_rows, groups, HEAD_SIZE)
    fresh_score = jnp.einsum(
        "rgqd,rgd->rgq", grouped_queries, new_keys, preferred_element_type=jnp.float32
    ).reshape(own_rows, heads) * (1.0 / math.sqrt(HEAD_SIZE))
    top_score = jnp.maximum(cache_max, fresh_score)
    carried = jnp.exp(cache_max - top_score)
    own_weight = jnp.exp(fresh_score - top_score)
    denominator = own_weight + cache_total * carried
    new_values = jnp.broadcast_to(
        fresh_key_value[1].astype(jnp.float32).reshape(own_rows, groups, 1, HEAD_SIZE),
        (own_rows, groups, per_group, HEAD_SIZE),
    ).reshape(own_rows, heads, HEAD_SIZE)
    weighted = (
        own_weight[:, :, None] * new_values
        + cache_out.reshape(own_rows, heads, HEAD_SIZE) * carried[:, :, None]
    )
    return (
        (weighted / denominator[:, :, None])
        .reshape(own_rows, heads * HEAD_SIZE)
        .astype(jnp.bfloat16)
    )


def shards(queries, fresh_key_value, key_value_pool, block_table, lengths):
    all_tables, all_lengths = (
        lax.all_gather(block_table, "inst", axis=0, tiled=True),
        lax.all_gather(lengths, "inst", axis=0, tiled=True),
    )
    all_queries = lax.all_gather(queries, "inst", axis=0, tiled=True)
    requests = all_tables.shape[0]
    own_rows = queries.shape[0]
    row_start = lax.axis_index("inst") * own_rows
    page_owner, filled = slot_owners(
        all_tables, all_lengths, key_value_pool.shape[1], key_value_pool.shape[2]
    )
    slot_queries = all_queries[jnp.minimum(page_owner, requests - 1)]
    page_max, page_sum, page_out = page_partials(slot_queries, key_value_pool, filled)
    local_max = request_max(page_max, page_owner, requests)
    shared_max = lax.pmax(local_max, ("inst", "page"))
    shared_total, shared_out = request_sums(page_max, page_sum, page_out, page_owner, shared_max)
    summed_out, summed_total = lax.psum((shared_out, shared_total), ("inst", "page"))
    cache_max = lax.dynamic_slice_in_dim(shared_max, row_start, own_rows, 0)
    cache_total = lax.dynamic_slice_in_dim(summed_total, row_start, own_rows, 0)
    cache_out = lax.dynamic_slice_in_dim(summed_out, row_start, own_rows, 0)
    return finish(queries, fresh_key_value, cache_max, cache_total, cache_out)


def solution(mesh):
    return jax.shard_map(
        shards,
        mesh=mesh,
        in_specs=(
            P("inst", "head"),
            P(None, "inst", "head"),
            P(None, ("inst", "page"), None, "head"),
            P("inst", None),
            P("inst"),
        ),
        out_specs=P("inst", "head"),
        check_vma=False,
    )
```

profile of v0, /device:TPU:8, one launch (start us, length us, event | category | flops | bytes accessed | tf_op | source)
XLA Modules:
  0.0 1645.3 jit_solution(2714726597789726109)
XLA Ops:
  6.5 1.3 dynamic-slice
  8.5 0.9 dynamic-update-slice
  9.3 15.6 all-reduce.1
  24.9 21.9 %all-gather = s32[16,2,768]{2,1,0:T(2,128)S(1)} all-gather(s32[1,2,768]{2,1,0:T(2,128)} %bitcast.89), channel_id=1, replica_groups=mesh['inst'=16,'page'=8,'head'=2] {'inst'}, dimensions={0}, use_global_device_ids=true | all-gather | bytes 104448 | tf_op jit(solution)/shard_map/all_gather | solution.py:122
  47.2 90.2 %scatter_custom_fusion = s32[128]{0:T(128)S(1)} fusion(s32[24576]{0:T(1024)S(1)} %bitcast.84, s32[24576]{0:T(1024)S(1)} %reshape.155, s32[]{:T(128)} %constant.17.clone.1), kind=kCustom, calls=%fused_computation.59 | custom fusion | bytes 516 | tf_op jit(solution)/shard_map/scatter | solution.py:27
  137.4 90.2 %scatter_custom_fusion.1 = s32[128]{0:T(128)S(1)} fusion(s32[24576]{0:T(1024)S(1)} %bitcast.85, s32[24576]{0:T(1024)S(1)} %reshape.163, s32[]{:T(128)} %constant.5.clone.1), kind=kCustom, calls=%fused_computation.57 | custom fusion | bytes 516 | tf_op jit(solution)/shard_map/scatter | solution.py:29
  227.7 21.7 %all-gather.1 = bf16[16,2,4096]{2,1,0:T(2,128)(2,1)S(1)} all-gather(bf16[1,2,4096]{2,1,0:T(2,128)(2,1)} %bitcast.87), channel_id=1, replica_groups=mesh['inst'=16,'page'=8,'head'=2] {'inst'}, dimensions={0}, use_global_device_ids=true | all-gather | bytes 278528 | tf_op jit(solution)/shard_map/all_gather | solution.py:125
  249.6 1.2 gather_fusion
  250.8 0.2 copy.37
  251.0 4.6 fusion.34
  255.6 3.5 copy.34
  259.1 3.0 copy.27
  262.1 3.5 copy.33
  265.6 3.0 copy.24
  268.5 2.9 fusion.4
  271.9 670.8 %pmax.7 = f32[32,32]{1,0:T(8,128)S(1)} all-reduce(f32[32,32]{1,0:T(8,128)S(1)} %select_reduce_fusion), channel_id=1, replica_groups=mesh['inst'=16,'page'=8,'head'=2] {'inst','page'}, use_global_device_ids=true, to_apply=%region_4.5 | all-reduce | flops 1024 | bytes 8192 | tf_op jit(solution)/shard_map/pmax | solution.py:135
  942.7 3.7 fusion.7
  946.4 0.6 gather_fusion.1
  947.1 0.6 mul.86
  947.7 1.0 copy-done
  948.7 4.3 fusion
  953.0 1.4 fusion.5
  955.0 681.6 %psum.15 = f32[32,32]{1,0:T(8,128)S(1)} all-reduce(f32[32,32]{1,0:T(8,128)S(1)} %fusion.14), channel_id=1, replica_groups=mesh['inst'=16,'page'=8,'head'=2] {'inst','page'}, use_global_device_ids=true, to_apply=%region_7.8 | all-reduce | flops 1024 | bytes 8192 | tf_op jit(solution)/shard_map/psum | solution.py:137
  1636.9 1.6 fusion.17
  (42 shorter events, 1.9 us)
Async XLA Ops:
  6.5 1630.3 %all-reduce.4.cloned.1.call-start = ((), (), s32[]{:S(2)}) async-start(), calls=%async_computation | async-start | bytes 1048576 | tf_op jit(solution)/shard_map/psum | solution.py:137
  947.1 1.6 copy-start
  953.0 1.4 copy-start.2
  953.0 1.4 copy-start.1
Sparse Core Ops, SparseCore 0:
  953.2 227.6 all-reduce.3
where the time goes:
time: 1660 us; the launch traced here: 1650 us
  blocking collectives  1410 us (85%)
  local copies, waits for them, and re-layouts  205 us (12%)
    psum x1, blocking collectives, shards(): lax.psum((shared_out, shared_total), ('inst', 'page'))  682 us
    pmax x1, blocking collectives, shards(): shared_max = lax.pmax(local_max, ('inst', 'page'))  671 us
    scatter x1, local copies, waits for them, and re-layouts, slot_owners(): jnp.full((slots,), requests, jnp.int32).at[expected_output]  90.2 us
    scatter x1, local copies, waits for them, and re-layouts, slot_owners(): jnp.zeros((slots,), jnp.int32).at[expected_output]  90.2 us
  transfers between devices with their start and end apart: 1, of which 0 were waited for; matrix products, arithmetic and copies ran while one was open for 0% of the time, Pallas kernels for 0%

commit v1 on v0

v1 whole, which is shorter than its diff:
```python
import functools
import math

import jax
import jax.numpy as jnp
from jax import lax
from jax.experimental import pallas as pl
from jax.experimental.pallas import tpu as pltpu
from jax.sharding import PartitionSpec as P

HEAD_SIZE = 128
LOWEST_SCORE = -1e30
SCALE = 1.0 / math.sqrt(HEAD_SIZE)
VMEM = pltpu.MemorySpace.VMEM
SMEM = pltpu.MemorySpace.SMEM
f32 = jnp.float32
bf16 = jnp.bfloat16


def nt_dot(a, b):
    return lax.dot_general(a, b, (((1,), (1,)), ((), ())), preferred_element_type=f32)


def vmem_specs(n):
    return [pl.BlockSpec(memory_space=VMEM)] * n


def send_kernel(slots, pages, page_ref, lengths_ref, queries_ref, table_ref, out_ref):
    peers = out_ref.shape[0]
    own_rows, most_pages = table_ref.shape
    page_tok = 16
    column = lax.broadcasted_iota(jnp.int32, (1, most_pages), 1)
    fills = []
    for row in range(own_rows):
        entry = table_ref[row : row + 1, :]
        fill = jnp.clip(lengths_ref[row] - column * page_tok, 0, page_tok)
        here = (entry // slots) % pages == page_ref[0]
        fill = jnp.where(here & (entry >= 0), fill, 0)
        lender = entry // (slots * pages)
        slot = entry % slots
        lender_rows = lax.broadcasted_iota(jnp.int32, (peers, most_pages), 0)
        slot_rows = lax.broadcasted_iota(jnp.int32, (slots, most_pages), 0)
        a = jnp.where(lender_rows == lender, fill, 0).astype(f32).astype(bf16)
        b = jnp.where(slot_rows == slot, 1.0, 0.0).astype(bf16)
        fills.append(nt_dot(a, b))
    sub = lax.broadcasted_iota(jnp.int32, (16, slots), 0)
    rows = queries_ref.shape[0]
    queries = queries_ref[...]
    for peer in range(peers):
        out_ref[peer, 0:rows, :] = queries
        tile = jnp.zeros((16, slots), f32)
        for row in range(own_rows):
            tile = jnp.where(sub == row, fills[row][peer : peer + 1, :], tile)
        out_ref[peer, rows : rows + 16, :] = tile.astype(bf16)


def token_major_kernel(pool_ref, out_ref):
    pages, page_tok, width = pool_ref.shape[1:]
    block = page_tok * 16
    i = lax.broadcasted_iota(jnp.int32, (block, block), 0)
    j = lax.broadcasted_iota(jnp.int32, (block, block), 1)
    perm = jnp.where((i % 16) * page_tok + i // 16 == j, 1.0, 0.0).astype(bf16)
    for b in range(pages // 16):
        rows = pool_ref[0, b * 16 : (b + 1) * 16].reshape(block, width)
        moved = jnp.dot(perm, rows, preferred_element_type=f32).astype(bf16)
        out_ref[0, :, b * 16 : (b + 1) * 16, :] = moved.reshape(page_tok, 16, width)


def attend_kernel(recv_ref, kv_ref, out_ref, score_ref, weight_ref):
    peers = recv_ref.shape[0]
    page_tok, slots, width = kv_ref.shape[1:]
    groups = width // HEAD_SIZE
    requests = 2 * peers
    heads = groups * 8
    rows = groups * 16
    sub8 = lax.broadcasted_iota(jnp.int32, (8, slots), 0)
    fill = jnp.zeros((8, slots), f32)
    code = jnp.zeros((8, slots), f32)
    for peer in range(peers):
        tile = recv_ref[peer, rows : rows + 16, :].astype(f32)[0:8]
        fill = fill + tile
        code = code + jnp.where(tile > 0.0, (sub8 + (2 * peer + 1)).astype(f32), 0.0)
    fill = jnp.broadcast_to(jnp.sum(fill, axis=0, keepdims=True), (8, slots))
    owner = jnp.broadcast_to(jnp.sum(code, axis=0, keepdims=True), (8, slots))

    def score_step(t, carry):
        live = fill > t.astype(f32)
        for g in range(groups):
            q = recv_ref[:, g * 16 : (g + 1) * 16, :].reshape(requests * 8, HEAD_SIZE)
            k = kv_ref[0, t, :, g * HEAD_SIZE : (g + 1) * HEAD_SIZE]
            s = nt_dot(q, k)
            picked = jnp.zeros((8, slots), f32)
            for r in range(requests):
                picked = jnp.where(owner == float(r + 1), s[r * 8 : (r + 1) * 8], picked)
            score_ref[t, g * 8 : (g + 1) * 8, :] = jnp.where(live, picked * SCALE, LOWEST_SCORE)
        return carry

    lax.fori_loop(0, page_tok, score_step, 0)

    owner_h = jnp.broadcast_to(owner[0:1], (heads, slots))
    fill_h = jnp.broadcast_to(fill[0:1], (heads, slots))
    page_max = score_ref[0]
    for t in range(1, page_tok):
        page_max = jnp.maximum(page_max, score_ref[t])
    maxima = []
    owner_max = jnp.zeros((heads, slots), f32)
    for r in range(requests):
        mine = owner_h == float(r + 1)
        top = jnp.max(jnp.where(mine, page_max, LOWEST_SCORE), axis=1, keepdims=True)
        maxima.append(top)
        owner_max = jnp.where(mine, top, owner_max)
    factor = jnp.exp(page_max - owner_max)
    page_sum = jnp.zeros((heads, slots), f32)
    sub16 = lax.broadcasted_iota(jnp.int32, (16, slots), 0)
    owner_16 = jnp.broadcast_to(owner[0:1], (16, slots))
    for t in range(page_tok):
        w = jnp.where(fill_h > float(t), jnp.exp(score_ref[t] - page_max), 0.0)
        page_sum = page_sum + w
        scaled = w.astype(bf16).astype(f32) * factor
        high = scaled.astype(bf16).astype(f32)
        score_ref[t] = high
        weight_ref[t] = scaled - high
    page_sum = page_sum * factor
    masks = [
        jnp.where(owner_16 == (2 * k + 1 + sub16 // 8).astype(f32), 1.0, 0.0).astype(bf16)
        for k in range(peers)
    ]
    totals = [
        jnp.sum(jnp.where(owner_h == float(r + 1), page_sum, 0.0), axis=1, keepdims=True)
        for r in range(requests)
    ]
    lane = lax.broadcasted_iota(jnp.int32, (8, HEAD_SIZE), 1)
    for peer in range(peers):
        tile = jnp.zeros((8, HEAD_SIZE), f32)
        for g in range(groups):
            for row in range(2):
                r = 2 * peer + row
                c = g * 2 + row
                tile = jnp.where(lane == c, maxima[r][g * 8 : (g + 1) * 8], tile)
                tile = jnp.where(lane == 2 * groups + c, totals[r][g * 8 : (g + 1) * 8], tile)
        out_ref[peer, rows : rows + 8, :] = tile
    for g in range(groups):
        acc = jnp.zeros((requests * 8, HEAD_SIZE), f32)
        for t0 in range(0, page_tok, 2):
            v = kv_ref[1, t0 : t0 + 2, :, g * HEAD_SIZE : (g + 1) * HEAD_SIZE].reshape(
                2 * slots, HEAD_SIZE
            )
            for ref in (score_ref, weight_ref):
                cols = []
                for t in (t0, t0 + 1):
                    w8 = ref[t, g * 8 : (g + 1) * 8, :]
                    w16 = jnp.concatenate([w8, w8], axis=0).astype(bf16)
                    cols.append(jnp.concatenate([w16 * m for m in masks], axis=0))
                acc = acc + jnp.dot(
                    jnp.concatenate(cols, axis=1), v, preferred_element_type=f32
                )
        out_ref[:, g * 16 : (g + 1) * 16, :] = acc.reshape(peers, 16, HEAD_SIZE)


def merge(parts_ref, groups):
    tiles = 2 * groups
    count = parts_ref.shape[0]
    stats = [parts_ref[i, tiles * 8 : tiles * 8 + 8, :] for i in range(count)]
    top = stats[0]
    for s in stats[1:]:
        top = jnp.maximum(top, s)
    scales = [jnp.exp(s - top) for s in stats]
    total = jnp.zeros_like(top)
    for s, e in zip(stats, scales):
        total = total + pltpu.roll(s, HEAD_SIZE - tiles, axis=1) * e
    sums = []
    for c in range(tiles):
        acc = jnp.zeros((8, HEAD_SIZE), f32)
        for i in range(count):
            acc = acc + parts_ref[i, c * 8 : (c + 1) * 8, :] * scales[i][:, c : c + 1]
        sums.append(acc)
    return top, total, sums


def combine_kernel(groups, parts_ref, out_ref):
    tiles = 2 * groups
    top, total, sums = merge(parts_ref, groups)
    lane = lax.broadcasted_iota(jnp.int32, (8, HEAD_SIZE), 1)
    stat = jnp.where(lane < tiles, top, pltpu.roll(total, tiles, axis=1))
    for i in range(out_ref.shape[0]):
        for c in range(tiles):
            out_ref[i, c * 8 : (c + 1) * 8, :] = sums[c]
        out_ref[i, tiles * 8 : tiles * 8 + 8, :] = stat


def finish_kernel(groups, parts_ref, queries_ref, fresh_ref, out_ref):
    top, total, sums = merge(parts_ref, groups)
    fresh_k = fresh_ref[0].astype(f32)
    fresh_v = fresh_ref[1].astype(f32)
    for g in range(groups):
        outs = []
        q2 = queries_ref[g * 16 : (g + 1) * 16, :].astype(f32)
        for row in range(2):
            c = g * 2 + row
            k = fresh_k[row : row + 1, g * HEAD_SIZE : (g + 1) * HEAD_SIZE]
            v = fresh_v[row : row + 1, g * HEAD_SIZE : (g + 1) * HEAD_SIZE]
            new = jnp.sum(q2[row * 8 : row * 8 + 8] * k, axis=1, keepdims=True) * SCALE
            cache = top[:, c : c + 1]
            best = jnp.maximum(cache, new)
            carried = jnp.exp(cache - best)
            own = jnp.exp(new - best)
            denominator = own + total[:, c : c + 1] * carried
            outs.append((own * v + sums[c] * carried) / denominator)
        out_ref[g * 16 : (g + 1) * 16, :] = jnp.concatenate(outs, axis=0).astype(bf16)


def shards(queries, fresh_key_value, key_value_pool, block_table, lengths):
    lenders = lax.axis_size("inst")
    pages = lax.axis_size("page")
    own_rows = queries.shape[0]
    slots, page_tok, width = key_value_pool.shape[1:]
    groups = width // HEAD_SIZE
    rows = groups * 16
    q = (
        queries.reshape(own_rows, groups, 8, HEAD_SIZE)
        .transpose(1, 0, 2, 3)
        .reshape(rows, HEAD_SIZE)
    )
    page_index = lax.axis_index("page").reshape(1).astype(jnp.int32)

    to_send = pl.pallas_call(
        functools.partial(send_kernel, slots, pages),
        out_shape=jax.ShapeDtypeStruct((lenders, rows + 16, HEAD_SIZE), bf16),
        in_specs=[pl.BlockSpec(memory_space=SMEM)] * 2 + vmem_specs(2),
        out_specs=pl.BlockSpec(memory_space=VMEM),
        name="send",
    )(page_index, lengths, q, block_table)
    received = lax.all_to_all(to_send, "inst", 0, 0)

    kv = pl.pallas_call(
        token_major_kernel,
        grid=(2, 2),
        out_shape=jax.ShapeDtypeStruct((2, page_tok, slots, width), bf16),
        in_specs=[pl.BlockSpec((1, slots // 2, page_tok, width), lambda i, j: (i, j, 0, 0))],
        out_specs=pl.BlockSpec((1, page_tok, slots // 2, width), lambda i, j: (i, 0, j, 0)),
        cost_estimate=pl.CostEstimate(flops=10**9, bytes_accessed=2 * 4 * 2**20, transcendentals=0),
        name="token_major",
    )(key_value_pool)

    partial = pl.pallas_call(
        attend_kernel,
        out_shape=jax.ShapeDtypeStruct((lenders, rows + 8, HEAD_SIZE), f32),
        in_specs=vmem_specs(2),
        out_specs=pl.BlockSpec(memory_space=VMEM),
        scratch_shapes=[
            pltpu.VMEM((page_tok, groups * 8, slots), f32),
            pltpu.VMEM((page_tok, groups * 8, slots), f32),
        ],
        name="attend",
    )(received, kv)
    parts = lax.all_to_all(partial, "inst", 0, 0)

    combined = pl.pallas_call(
        functools.partial(combine_kernel, groups),
        out_shape=jax.ShapeDtypeStruct((pages, rows + 8, HEAD_SIZE), f32),
        in_specs=vmem_specs(1),
        out_specs=pl.BlockSpec(memory_space=VMEM),
        name="combine",
    )(parts)
    page_parts = lax.all_to_all(combined, "page", 0, 0)

    out = pl.pallas_call(
        functools.partial(finish_kernel, groups),
        out_shape=jax.ShapeDtypeStruct((rows, HEAD_SIZE), bf16),
        in_specs=vmem_specs(3),
        out_specs=pl.BlockSpec(memory_space=VMEM),
        name="finish",
    )(page_parts, q, fresh_key_value)
    return (
        out.reshape(groups, own_rows, 8, HEAD_SIZE)
        .transpose(1, 0, 2, 3)
        .reshape(own_rows, groups * 8 * HEAD_SIZE)
    )


def solution(mesh):
    return jax.shard_map(
        shards,
        mesh=mesh,
        in_specs=(
            P("inst", "head"),
            P(None, "inst", "head"),
            P(None, ("inst", "page"), None, "head"),
            P("inst", None),
            P("inst"),
        ),
        out_specs=P("inst", "head"),
        check_vma=False,
    )
```

time: 1660 us -> 69.5 us (0.04)
  blocking collectives: 1410 us -> 35 us
  local copies, waits for them, and re-layouts: 205 us -> 3.4 us
  Pallas kernels: 0 us -> 20.9 us
    psum x1 -> x0, blocking collectives: 682 us -> none  [shards(): lax.psum((shared_out, shared_total), ('inst', 'page'))]
    pmax x1 -> x0, blocking collectives: 671 us -> none  [shards(): shared_max = lax.pmax(local_max, ('inst', 'page'))]
    scatter x2 -> x0, local copies, waits for them, and re-layouts: 180 us -> none  [the longest x1 90.2 us: slot_owners(): jnp.full((slots,), requests, jnp.int32).at[expected_output]]
    all_gather x2 -> x0, blocking collectives: 43.7 us -> none  [the longest x1 21.9 us: shards(): lax.all_gather(block_table, 'inst', axis=0, tiled=True)]
    all_to_all x0 -> x2, blocking collectives: none -> 35 us  [the longest x1 19.4 us: shards(): page_parts = lax.all_to_all(combined, 'page', 0, 0)]
    pallas_call x0 -> x5, Pallas kernels: none -> 20.9 us  [the longest x1 9.42 us: shards(): pl.pallas_call(attend_kernel, out_shape=jax.ShapeDtypeStruct((lenders, ro...]
  transfers between devices with their start and end apart: 1 -> 1, of which waited for: 0 -> 1; matrix products, arithmetic and copies ran while one was open for 0% -> 0% of each run, Pallas kernels for 0% -> 8%
where the time goes in v1:
time: 69.5 us; the launch traced here: 68.7 us
  blocking collectives  35 us (50%)
  Pallas kernels  20.9 us (30%)
  starting transfers between devices  7.39 us (11%)
  local copies, waits for them, and re-layouts  3.4 us (5%)
  waiting for transfers between devices  2.07 us (3%)
    all_to_all x1, blocking collectives, shards(): page_parts = lax.all_to_all(combined, 'page', 0, 0)  19.4 us
    all_to_all x1, blocking collectives, shards(): parts = lax.all_to_all(partial, 'inst', 0, 0)  15.6 us
    pallas_call x1, Pallas kernels, shards(): pl.pallas_call(attend_kernel, out_shape=jax.ShapeDtypeStruct((lenders, ro...  9.42 us
    all_to_all x1, starting transfers between devices, shards(): received = lax.all_to_all(to_send, 'inst', 0, 0)  7.39 us
    pallas_call x1, Pallas kernels, shards(): pl.pallas_call(token_major_kernel, grid=(2, 2), out_shape=jax.ShapeDtypeS...  5.59 us
    pallas_call x1, Pallas kernels, shards(): pl.pallas_call(functools.partial(finish_kernel, groups), out_shape=jax.Sh...  2.17 us
    unnamed x4, local copies, waits for them, and re-layouts  2.08 us
    all_to_all x1, waiting for transfers between devices, shards(): received = lax.all_to_all(to_send, 'inst', 0, 0)  2.07 us
  transfers between devices with their start and end apart: 1, of which 1 were waited for; matrix products, arithmetic and copies ran while one was open for 0% of the time, Pallas kernels for 8%

profile of v1, /device:TPU:8, one launch (start us, length us, event | category | flops | bytes accessed | tf_op | source)
XLA Modules:
  0.0 68.7 jit_solution(16416147767268227403)
XLA Ops:
  0.0 0.7 %copy.14 = bf16[1,2,32,128]{3,2,1,0:T(8,128)(2,1)S(1)} copy(bf16[1,2,32,128]{3,1,2,0:T(2,128)(2,1)} %bitcast.24) | data formatting | bytes 32768
  0.7 0.6 copy.6
  1.3 1.7 %send.1 = bf16[16,80,128]{2,1,0:T(8,128)(2,1)} custom-call(s32[1]{0:T(128)} %bitcast.page_ref, s32[2]{0:T(128)} %lengths_ref.1, bf16[64,128]{1,0:T(8,128)(2,1)} %bitcast.19, s32[2,768]{1,0:T(2,128)} %table_ref.1), custom_call_target="tpu_custom_call" | custom-call | tf_op jit(solution)/shard_map/send/pallas_call | solution.py:226
  3.0 7.4 %all-to-all-start = ((bf16[16,80,128]{2,1,0:T(8,128)(2,1)}), bf16[16,80,128]{2,1,0:T(8,128)(2,1)S(1)}, u32[]{:S(2)}, u32[]{:S(2)}) async-start(bf16[16,80,128]{2,1,0:T(8,128)(2,1)} %send.1), calls=%async_computation | async-start | bytes 655360 | tf_op jit(solution)/shard_map/all_to_all | solution.py:233
  10.4 5.6 %token_major.1.kv_ref = bf16[2,16,128,512]{3,2,1,0:T(8,128)(2,1)} custom-call(bf16[2,128,16,512]{3,2,1,0:T(8,128)(2,1)} %pool_ref.1), custom_call_target="tpu_custom_call" | custom-call | flops 1000000000 | bytes 8388608 | tf_op jit(solution)/shard_map/token_major/pallas_call | solution.py:235
  16.0 2.1 %all-to-all-done.recv_ref = bf16[16,80,128]{2,1,0:T(8,128)(2,1)S(1)} async-done(((bf16[16,80,128]{2,1,0:T(8,128)(2,1)}), bf16[16,80,128]{2,1,0:T(8,128)(2,1)S(1)}, u32[]{:S(2)}, u32[]{:S(2)}) %all-to-all-start) | async-done | bytes 327712 | tf_op jit(solution)/shard_map/all_to_all | solution.py:233
  18.1 0.0 copy-start
  18.1 0.7 %copy-done = bf16[16,80,128]{2,1,0:T(8,128)(2,1)} copy-done((bf16[16,80,128]{2,1,0:T(8,128)(2,1)}, bf16[16,80,128]{2,1,0:T(8,128)(2,1)S(1)}, u32[]{:S(2)}) %copy-start) | copy-done | bytes 327704
  18.8 9.4 %attend.1 = f32[16,72,128]{2,1,0:T(8,128)} custom-call(bf16[16,80,128]{2,1,0:T(8,128)(2,1)} %copy-done, bf16[2,16,128,512]{3,2,1,0:T(8,128)(2,1)} %token_major.1.kv_ref), custom_call_target="tpu_custom_call" | custom-call | tf_op jit(solution)/shard_map/attend/pallas_call | solution.py:245
  28.2 15.6 %all_to_all.15.parts_ref = f32[16,72,128]{2,1,0:T(8,128)} all-to-all(f32[16,72,128]{2,1,0:T(8,128)} %attend.1), channel_id=1, replica_groups=mesh['inst'=16,'page'=8,'head'=2] {'inst'}, dimensions={0} | all-to-all | bytes 1179648 | tf_op jit(solution)/shard_map/all_to_all | solution.py:256
  43.8 2.0 %combine.1 = f32[8,72,128]{2,1,0:T(8,128)} custom-call(f32[16,72,128]{2,1,0:T(8,128)} %all_to_all.15.parts_ref), custom_call_target="tpu_custom_call" | custom-call | tf_op jit(solution)/shard_map/combine/pallas_call | solution.py:258
  45.8 19.4 %all_to_all.16.parts_ref = f32[8,72,128]{2,1,0:T(8,128)} all-to-all(f32[8,72,128]{2,1,0:T(8,128)} %combine.1), channel_id=1, replica_groups=mesh['inst'=16,'page'=8,'head'=2] {'page'}, dimensions={0} | all-to-all | bytes 589824 | tf_op jit(solution)/shard_map/all_to_all | solution.py:265
  65.2 2.2 %finish.1 = bf16[64,128]{1,0:T(8,128)(2,1)} custom-call(f32[8,72,128]{2,1,0:T(8,128)} %all_to_all.16.parts_ref, bf16[64,128]{1,0:T(8,128)(2,1)} %bitcast.20, bf16[2,2,512]{2,1,0:T(2,128)(2,1)} %fresh_ref.1), custom_call_target="tpu_custom_call" | custom-call | tf_op jit(solution)/shard_map/finish/pallas_call | solution.py:267
  67.4 0.7 %copy.15 = bf16[2,4,8,128]{3,2,1,0:T(8,128)(2,1)S(1)} copy(bf16[2,4,8,128]{3,2,0,1:T(8,128)(2,1)} %bitcast.23) | data formatting | bytes 32768 | tf_op jit(solution)/shard_map/transpose | solution.py:276
  68.1 0.6 copy.13
Async XLA Ops:
  3.0 15.0 %all-to-all-start = ((bf16[16,80,128]{2,1,0:T(8,128)(2,1)}), bf16[16,80,128]{2,1,0:T(8,128)(2,1)S(1)}, u32[]{:S(2)}, u32[]{:S(2)}) async-start(bf16[16,80,128]{2,1,0:T(8,128)(2,1)} %send.1), calls=%async_computation | async-start | bytes 655360 | tf_op jit(solution)/shard_map/all_to_all | solution.py:233
  18.1 0.7 %copy-start = (bf16[16,80,128]{2,1,0:T(8,128)(2,1)}, bf16[16,80,128]{2,1,0:T(8,128)(2,1)S(1)}, u32[]{:S(2)}) copy-start(bf16[16,80,128]{2,1,0:T(8,128)(2,1)S(1)} %all-to-all-done.recv_ref) | copy-start | bytes 983044

commit v2 on v1

--- a/solution.py
+++ b/solution.py
@@ -28,24 +28,37 @@
 def send_kernel(slots, pages, page_ref, lengths_ref, queries_ref, table_ref, out_ref):
     peers = out_ref.shape[0]
     own_rows, most_pages = table_ref.shape
+    heads = queries_ref.shape[1] // HEAD_SIZE
     page_tok = 16
+    slot_bits = slots.bit_length() - 1
+    page_bits = pages.bit_length() - 1
     column = lax.broadcasted_iota(jnp.int32, (1, most_pages), 1)
+    lender_rows = lax.broadcasted_iota(jnp.int32, (peers, most_pages), 0)
+    slot_rows = lax.broadcasted_iota(jnp.int32, (slots, most_pages), 0)
     fills = []
     for row in range(own_rows):
         entry = table_ref[row : row + 1, :]
         fill = jnp.clip(lengths_ref[row] - column * page_tok, 0, page_tok)
-        here = (entry // slots) % pages == page_ref[0]
-        fill = jnp.where(here & (entry >= 0), fill, 0)
-        lender = entry // (slots * pages)
-        slot = entry % slots
-        lender_rows = lax.broadcasted_iota(jnp.int32, (peers, most_pages), 0)
-        slot_rows = lax.broadcasted_iota(jnp.int32, (slots, most_pages), 0)
-        a = jnp.where(lender_rows == lender, fill, 0).astype(f32).astype(bf16)
+        here = ((entry >> slot_bits) & (pages - 1)) == page_ref[0]
+        lender = jnp.where(here & (entry >= 0), entry >> (slot_bits + page_bits), -1)
+        slot = entry & (slots - 1)
+        a = jnp.where(lender_rows == lender, fill.astype(f32), 0.0).astype(bf16)
         b = jnp.where(slot_rows == slot, 1.0, 0.0).astype(bf16)
         fills.append(nt_dot(a, b))
+    sub = lax.broadcasted_iota(jnp.int32, (8, HEAD_SIZE), 0)
+    pieces = []
+    for g in range(heads // 8):
+        pair = [jnp.zeros((8, HEAD_SIZE), f32)] * own_rows
+        for head in range(8):
+            at = (g * 8 + head) * HEAD_SIZE
+            both = queries_ref[:, at : at + HEAD_SIZE].astype(f32)
+            pair = [
+                jnp.where(sub == head, both[row : row + 1, :], pair[row]) for row in range(own_rows)
+            ]
+        pieces += pair
+    queries = jnp.concatenate(pieces, axis=0).astype(bf16)
+    rows = own_rows * heads
     sub = lax.broadcasted_iota(jnp.int32, (16, slots), 0)
-    rows = queries_ref.shape[0]
-    queries = queries_ref[...]
     for peer in range(peers):
         out_ref[peer, 0:rows, :] = queries
         tile = jnp.zeros((16, slots), f32)
@@ -66,9 +79,27 @@
         out_ref[0, :, b * 16 : (b + 1) * 16, :] = moved.reshape(page_tok, 16, width)
 
 
-def attend_kernel(recv_ref, kv_ref, out_ref, score_ref, weight_ref):
+CHUNKS = 4
+
+
+def attend_kernel(recv_ref, kv_hbm, out_ref, kv_ref, score_ref, weight_ref, sems):
     peers = recv_ref.shape[0]
     page_tok, slots, width = kv_ref.shape[1:]
+    step = page_tok // CHUNKS
+    loads = [
+        [
+            pltpu.make_async_copy(
+                kv_hbm.at[kind, pl.ds(c * step, step)],
+                kv_ref.at[kind, pl.ds(c * step, step)],
+                sems.at[kind, c],
+            )
+            for c in range(CHUNKS)
+        ]
+        for kind in range(2)
+    ]
+    for kind in range(2):
+        for c in range(CHUNKS):
+            loads[kind][c].start()
     groups = width // HEAD_SIZE
     requests = 2 * peers
     heads = groups * 8
@@ -84,7 +115,7 @@
     owner = jnp.broadcast_to(jnp.sum(code, axis=0, keepdims=True), (8, slots))
 
     def score_step(t, carry):
-        live = fill > t.astype(f32)
+        live = fill > jnp.asarray(t, f32)
         for g in range(groups):
             q = recv_ref[:, g * 16 : (g + 1) * 16, :].reshape(requests * 8, HEAD_SIZE)
             k = kv_ref[0, t, :, g * HEAD_SIZE : (g + 1) * HEAD_SIZE]
@@ -95,7 +126,9 @@
             score_ref[t, g * 8 : (g + 1) * 8, :] = jnp.where(live, picked * SCALE, LOWEST_SCORE)
         return carry
 
-    lax.fori_loop(0, page_tok, score_step, 0)
+    for c in range(CHUNKS):
+        loads[0][c].wait()
+        lax.fori_loop(c * step, (c + 1) * step, score_step, 0, unroll=True)
 
     owner_h = jnp.broadcast_to(owner[0:1], (heads, slots))
     fill_h = jnp.broadcast_to(fill[0:1], (heads, slots))
@@ -139,6 +172,8 @@
                 tile = jnp.where(lane == c, maxima[r][g * 8 : (g + 1) * 8], tile)
                 tile = jnp.where(lane == 2 * groups + c, totals[r][g * 8 : (g + 1) * 8], tile)
         out_ref[peer, rows : rows + 8, :] = tile
+    for c in range(CHUNKS):
+        loads[1][c].wait()
     for g in range(groups):
         acc = jnp.zeros((requests * 8, HEAD_SIZE), f32)
         for t0 in range(0, page_tok, 2):
@@ -192,21 +227,32 @@
     top, total, sums = merge(parts_ref, groups)
     fresh_k = fresh_ref[0].astype(f32)
     fresh_v = fresh_ref[1].astype(f32)
+    sub = lax.broadcasted_iota(jnp.int32, (8, HEAD_SIZE), 0)
     for g in range(groups):
+        both = [
+            queries_ref[:, (g * 8 + h) * HEAD_SIZE : (g * 8 + h + 1) * HEAD_SIZE].astype(f32)
+            for h in range(8)
+        ]
         outs = []
-        q2 = queries_ref[g * 16 : (g + 1) * 16, :].astype(f32)
         for row in range(2):
             c = g * 2 + row
+            q = jnp.zeros((8, HEAD_SIZE), f32)
+            for h in range(8):
+                q = jnp.where(sub == h, both[h][row : row + 1, :], q)
             k = fresh_k[row : row + 1, g * HEAD_SIZE : (g + 1) * HEAD_SIZE]
             v = fresh_v[row : row + 1, g * HEAD_SIZE : (g + 1) * HEAD_SIZE]
-            new = jnp.sum(q2[row * 8 : row * 8 + 8] * k, axis=1, keepdims=True) * SCALE
+            new = jnp.sum(q * k, axis=1, keepdims=True) * SCALE
             cache = top[:, c : c + 1]
             best = jnp.maximum(cache, new)
             carried = jnp.exp(cache - best)
             own = jnp.exp(new - best)
             denominator = own + total[:, c : c + 1] * carried
             outs.append((own * v + sums[c] * carried) / denominator)
-        out_ref[g * 16 : (g + 1) * 16, :] = jnp.concatenate(outs, axis=0).astype(bf16)
+        for h in range(8):
+            at = (g * 8 + h) * HEAD_SIZE
+            out_ref[:, at : at + HEAD_SIZE] = jnp.concatenate(
+                [outs[0][h : h + 1], outs[1][h : h + 1]], axis=0
+            ).astype(bf16)
 
 
 def shards(queries, fresh_key_value, key_value_pool, block_table, lengths):
@@ -216,11 +262,6 @@
     slots, page_tok, width = key_value_pool.shape[1:]
     groups = width // HEAD_SIZE
     rows = groups * 16
-    q = (
-        queries.reshape(own_rows, groups, 8, HEAD_SIZE)
-        .transpose(1, 0, 2, 3)
-        .reshape(rows, HEAD_SIZE)
-    )
     page_index = lax.axis_index("page").reshape(1).astype(jnp.int32)
 
     to_send = pl.pallas_call(
@@ -228,8 +269,9 @@
         out_shape=jax.ShapeDtypeStruct((lenders, rows + 16, HEAD_SIZE), bf16),
         in_specs=[pl.BlockSpec(memory_space=SMEM)] * 2 + vmem_specs(2),
         out_specs=pl.BlockSpec(memory_space=VMEM),
+        compiler_params=pltpu.CompilerParams(vmem_limit_bytes=16 * 2**20),
         name="send",
-    )(page_index, lengths, q, block_table)
+    )(page_index, lengths, queries, block_table)
     received = lax.all_to_all(to_send, "inst", 0, 0)
 
     kv = pl.pallas_call(
@@ -245,12 +287,15 @@
     partial = pl.pallas_call(
         attend_kernel,
         out_shape=jax.ShapeDtypeStruct((lenders, rows + 8, HEAD_SIZE), f32),
-        in_specs=vmem_specs(2),
+        in_specs=vmem_specs(1) + [pl.BlockSpec(memory_space=pltpu.MemorySpace.HBM)],
         out_specs=pl.BlockSpec(memory_space=VMEM),
         scratch_shapes=[
+            pltpu.VMEM(kv.shape, bf16),
             pltpu.VMEM((page_tok, groups * 8, slots), f32),
             pltpu.VMEM((page_tok, groups * 8, slots), f32),
+            pltpu.SemaphoreType.DMA((2, CHUNKS)),
         ],
+        compiler_params=pltpu.CompilerParams(vmem_limit_bytes=52 * 2**20),
         name="attend",
     )(received, kv)
     parts = lax.all_to_all(partial, "inst", 0, 0)
@@ -260,22 +305,19 @@
         out_shape=jax.ShapeDtypeStruct((pages, rows + 8, HEAD_SIZE), f32),
         in_specs=vmem_specs(1),
         out_specs=pl.BlockSpec(memory_space=VMEM),
+        compiler_params=pltpu.CompilerParams(vmem_limit_bytes=16 * 2**20),
         name="combine",
     )(parts)
     page_parts = lax.all_to_all(combined, "page", 0, 0)
 
-    out = pl.pallas_call(
+    return pl.pallas_call(
         functools.partial(finish_kernel, groups),
-        out_shape=jax.ShapeDtypeStruct((rows, HEAD_SIZE), bf16),
+        out_shape=jax.ShapeDtypeStruct(queries.shape, bf16),
         in_specs=vmem_specs(3),
         out_specs=pl.BlockSpec(memory_space=VMEM),
+        compiler_params=pltpu.CompilerParams(vmem_limit_bytes=16 * 2**20),
         name="finish",
-    )(page_parts, q, fresh_key_value)
-    return (
-        out.reshape(groups, own_rows, 8, HEAD_SIZE)
-        .transpose(1, 0, 2, 3)
-        .reshape(own_rows, groups * 8 * HEAD_SIZE)
-    )
+    )(page_parts, queries, fresh_key_value)
 
 
 def solution(mesh):

time: 69.5 us -> 60.5 us (0.87)
  Pallas kernels: 20.9 us -> 14.1 us
  local copies, waits for them, and re-layouts: 3.4 us -> 2.07 us
    pallas_call x1, Pallas kernels: 9.42 us -> 5.57 us  [shards(): pl.pallas_call(attend_kernel, out_shape=jax.ShapeDtypeStruct((lenders, ro...]
    pallas_call x1, Pallas kernels: 2.03 us -> 0.25 us  [shards(): pl.pallas_call(functools.partial(combine_kernel, groups), out_shape=jax.S...]
    pallas_call x1, Pallas kernels: 2.17 us -> 1.2 us  [shards(): pl.pallas_call(functools.partial(finish_kernel, groups), out_shape=jax.Sh...]
    transpose x1 -> x0, local copies, waits for them, and re-layouts: 0.72 us -> none  [shards(): return out.reshape(groups, own_rows, 8, HEAD_SIZE).transpose(1, 0, 2, 3)....]
    unnamed x4 -> x10, local copies, waits for them, and re-layouts: 2.08 us -> 2.07 us
  transfers between devices with their start and end apart: 1 -> 1, of which waited for: 1 -> 1; matrix products, arithmetic and copies ran while one was open for 0% -> 0% of each run, Pallas kernels for 8% -> 9%
where the time goes in v2:
time: 60.5 us; the launch traced here: 60.1 us
  blocking collectives  34.4 us (57%)
  Pallas kernels  14.1 us (23%)
  starting transfers between devices  7.39 us (12%)
  waiting for transfers between devices  2.09 us (3%)
  local copies, waits for them, and re-layouts  2.07 us (3%)
    all_to_all x1, blocking collectives, shards(): page_parts = lax.all_to_all(combined, 'page', 0, 0)  19.1 us
    all_to_all x1, blocking collectives, shards(): parts = lax.all_to_all(partial, 'inst', 0, 0)  15.3 us
    all_to_all x1, starting transfers between devices, shards(): received = lax.all_to_all(to_send, 'inst', 0, 0)  7.39 us
    pallas_call x1, Pallas kernels, shards(): pl.pallas_call(attend_kernel, out_shape=jax.ShapeDtypeStruct((lenders, ro...  5.57 us
    pallas_call x1, Pallas kernels, shards(): pl.pallas_call(token_major_kernel, grid=(2, 2), out_shape=jax.ShapeDtypeS...  5.56 us
    all_to_all x1, waiting for transfers between devices, shards(): received = lax.all_to_all(to_send, 'inst', 0, 0)  2.09 us
    unnamed x10, local copies, waits for them, and re-layouts  2.07 us
    pallas_call x1, Pallas kernels, shards(): pl.pallas_call(functools.partial(send_kernel, slots, pages), out_shape=ja...  1.54 us
  transfers between devices with their start and end apart: 1, of which 1 were waited for; matrix products, arithmetic and copies ran while one was open for 0% of the time, Pallas kernels for 9%

profile of v2, /device:TPU:8, one launch (start us, length us, event | category | flops | bytes accessed | tf_op | source)
XLA Modules:
  0.0 60.1 jit_solution(1579679167258342606)
XLA Ops:
  0.0 0.0 copy-start
  0.0 0.7 %copy-done = bf16[2,4096]{1,0:T(2,128)(2,1)S(1)} copy-done((bf16[2,4096]{1,0:T(2,128)(2,1)S(1)}, bf16[2,4096]{1,0:T(2,128)(2,1)}, u32[]{:S(2)}) %copy-start) | copy-done | bytes 16408
  0.7 0.0 copy-start.2
  0.7 0.7 %copy-done.2 = s32[2,768]{1,0:T(2,128)S(1)} copy-done((s32[2,768]{1,0:T(2,128)S(1)}, s32[2,768]{1,0:T(2,128)}, u32[]{:S(2)}) %copy-start.2) | copy-done | bytes 6168
  1.4 0.0 copy-start.4
  1.4 0.7 %copy-done.4 = s32[2]{0:T(128)S(1)} copy-done((s32[2]{0:T(128)S(1)}, s32[2]{0:T(128)}, u32[]{:S(2)}) %copy-start.4) | copy-done | bytes 32
  2.1 1.5 %send.1 = bf16[16,80,128]{2,1,0:T(8,128)(2,1)} custom-call(s32[1]{0:T(128)} %bitcast.page_ref, s32[2]{0:T(128)S(1)} %copy-done.4, bf16[2,4096]{1,0:T(2,128)(2,1)S(1)} %copy-done, s32[2,768]{1,0:T(2,128)S(1)} %copy-done.2), custom_call_target="tpu_custom_call" | custom-call | tf_op jit(solution)/shard_map/send/pallas_call | solution.py:267
  3.6 7.4 %all-to-all-start = ((bf16[16,80,128]{2,1,0:T(8,128)(2,1)}), bf16[16,80,128]{2,1,0:T(8,128)(2,1)S(1)}, u32[]{:S(2)}, u32[]{:S(2)}) async-start(bf16[16,80,128]{2,1,0:T(8,128)(2,1)} %send.1), calls=%async_computation | async-start | bytes 655360 | tf_op jit(solution)/shard_map/all_to_all | solution.py:275
  11.0 5.6 %token_major.1.kv_hbm = bf16[2,16,128,512]{3,2,1,0:T(8,128)(2,1)} custom-call(bf16[2,128,16,512]{3,2,1,0:T(8,128)(2,1)} %pool_ref.1), custom_call_target="tpu_custom_call" | custom-call | flops 1000000000 | bytes 8388608 | tf_op jit(solution)/shard_map/token_major/pallas_call | solution.py:277
  16.6 0.0 copy-start.1
  16.6 0.0 copy-start.3
  16.6 2.1 %all-to-all-done.recv_ref = bf16[16,80,128]{2,1,0:T(8,128)(2,1)S(1)} async-done(((bf16[16,80,128]{2,1,0:T(8,128)(2,1)}), bf16[16,80,128]{2,1,0:T(8,128)(2,1)S(1)}, u32[]{:S(2)}, u32[]{:S(2)}) %all-to-all-start) | async-done | bytes 327712 | tf_op jit(solution)/shard_map/all_to_all | solution.py:275
  18.7 5.6 %attend.1 = f32[16,72,128]{2,1,0:T(8,128)S(1)} custom-call(bf16[16,80,128]{2,1,0:T(8,128)(2,1)S(1)} %all-to-all-done.recv_ref, bf16[2,16,128,512]{3,2,1,0:T(8,128)(2,1)} %token_major.1.kv_hbm), custom_call_target="tpu_custom_call" | custom-call | tf_op jit(solution)/shard_map/attend/pallas_call | solution.py:287
  24.2 15.3 %all_to_all.15.parts_ref = f32[16,72,128]{2,1,0:T(8,128)S(1)} all-to-all(f32[16,72,128]{2,1,0:T(8,128)S(1)} %attend.1), channel_id=1, replica_groups=mesh['inst'=16,'page'=8,'head'=2] {'inst'}, dimensions={0} | all-to-all | bytes 1179648 | tf_op jit(solution)/shard_map/all_to_all | solution.py:301
  39.5 0.2 combine.1
  39.7 19.1 %all_to_all.16.parts_ref = f32[8,72,128]{2,1,0:T(8,128)S(1)} all-to-all(f32[8,72,128]{2,1,0:T(8,128)S(1)} %combine.1), channel_id=1, replica_groups=mesh['inst'=16,'page'=8,'head'=2] {'page'}, dimensions={0} | all-to-all | bytes 589824 | tf_op jit(solution)/shard_map/all_to_all | solution.py:311
  58.8 0.0 copy-done.1
  58.8 0.0 copy-done.3
  58.9 1.2 %finish.1 = bf16[2,4096]{1,0:T(2,128)(2,1)} custom-call(f32[8,72,128]{2,1,0:T(8,128)S(1)} %all_to_all.16.parts_ref, bf16[2,4096]{1,0:T(2,128)(2,1)S(1)} %copy-done.1, bf16[2,2,512]{2,1,0:T(2,128)(2,1)S(1)} %copy-done.3), custom_call_target="tpu_custom_call" | custom-call | tf_op jit(solution)/shard_map/finish/pallas_call | solution.py:313
Async XLA Ops:
  0.0 0.7 %copy-start = (bf16[2,4096]{1,0:T(2,128)(2,1)S(1)}, bf16[2,4096]{1,0:T(2,128)(2,1)}, u32[]{:S(2)}) copy-start(bf16[2,4096]{1,0:T(2,128)(2,1)} %queries_ref.3) | copy-start | bytes 49156
  0.7 0.7 %copy-start.2 = (s32[2,768]{1,0:T(2,128)S(1)}, s32[2,768]{1,0:T(2,128)}, u32[]{:S(2)}) copy-start(s32[2,768]{1,0:T(2,128)} %table_ref.1) | copy-start | bytes 18436
  1.4 0.7 %copy-start.4 = (s32[2]{0:T(128)S(1)}, s32[2]{0:T(128)}, u32[]{:S(2)}) copy-start(s32[2]{0:T(128)} %lengths_ref.1) | copy-start | bytes 28
  3.6 15.0 %all-to-all-start = ((bf16[16,80,128]{2,1,0:T(8,128)(2,1)}), bf16[16,80,128]{2,1,0:T(8,128)(2,1)S(1)}, u32[]{:S(2)}, u32[]{:S(2)}) async-start(bf16[16,80,128]{2,1,0:T(8,128)(2,1)} %send.1), calls=%async_computation | async-start | bytes 655360 | tf_op jit(solution)/shard_map/all_to_all | solution.py:275
  16.6 42.3 %copy-start.1 = (bf16[2,4096]{1,0:T(2,128)(2,1)S(1)}, bf16[2,4096]{1,0:T(2,128)(2,1)}, u32[]{:S(2)}) copy-start(bf16[2,4096]{1,0:T(2,128)(2,1)} %queries_ref.3) | copy-start | bytes 49156
  16.6 42.3 %copy-start.3 = (bf16[2,2,512]{2,1,0:T(2,128)(2,1)S(1)}, bf16[2,2,512]{2,1,0:T(2,128)(2,1)}, u32[]{:S(2)}) copy-start(bf16[2,2,512]{2,1,0:T(2,128)(2,1)} %fresh_ref.1) | copy-start | bytes 12292

commit v3 on v2

--- a/solution.py
+++ b/solution.py
@@ -19,6 +19,19 @@
 
 def nt_dot(a, b):
     return lax.dot_general(a, b, (((1,), (1,)), ((), ())), preferred_element_type=f32)
+
+
+STEPS = 16.0
+FULL = 32700.0
+LOWEST_TOP = -32000.0
+PART = 32767.0
+
+
+def encode_rows(x):
+    top = jnp.max(jnp.abs(x), axis=1, keepdims=True)
+    k = jnp.ceil(jnp.log2(jnp.maximum(top, 2.0**-120)) * STEPS)
+    code = jnp.round((x * jnp.exp2(k * (-1.0 / STEPS))) * FULL)
+    return k, code.astype(jnp.int32).astype(jnp.int16)
 
 
 def vmem_specs(n):
@@ -139,7 +152,8 @@
     owner_max = jnp.zeros((heads, slots), f32)
     for r in range(requests):
         mine = owner_h == float(r + 1)
-        top = jnp.max(jnp.where(mine, page_max, LOWEST_SCORE), axis=1, keepdims=True)
+        top = jnp.max(jnp.where(mine, page_max, LOWEST_TOP), axis=1, keepdims=True)
+        top = jnp.round(jnp.maximum(top, LOWEST_TOP))
         maxima.append(top)
         owner_max = jnp.where(mine, top, owner_max)
     factor = jnp.exp(page_max - owner_max)
@@ -162,18 +176,9 @@
         jnp.sum(jnp.where(owner_h == float(r + 1), page_sum, 0.0), axis=1, keepdims=True)
         for r in range(requests)
     ]
-    lane = lax.broadcasted_iota(jnp.int32, (8, HEAD_SIZE), 1)
-    for peer in range(peers):
-        tile = jnp.zeros((8, HEAD_SIZE), f32)
-        for g in range(groups):
-            for row in range(2):
-                r = 2 * peer + row
-                c = g * 2 + row
-                tile = jnp.where(lane == c, maxima[r][g * 8 : (g + 1) * 8], tile)
-                tile = jnp.where(lane == 2 * groups + c, totals[r][g * 8 : (g + 1) * 8], tile)
-        out_ref[peer, rows : rows + 8, :] = tile
     for c in range(CHUNKS):
         loads[1][c].wait()
+    scales = []
     for g in range(groups):
         acc = jnp.zeros((requests * 8, HEAD_SIZE), f32)
         for t0 in range(0, page_tok, 2):
@@ -189,42 +194,89 @@
                 acc = acc + jnp.dot(
                     jnp.concatenate(cols, axis=1), v, preferred_element_type=f32
                 )
-        out_ref[:, g * 16 : (g + 1) * 16, :] = acc.reshape(peers, 16, HEAD_SIZE)
-
-
-def merge(parts_ref, groups):
+        k, code = encode_rows(acc)
+        scales.append(k)
+        out_ref[:, g * 16 : (g + 1) * 16, :] = code.reshape(peers, 16, HEAD_SIZE)
+    for peer in range(peers):
+        columns = []
+        for g in range(groups):
+            for row in range(2):
+                r = 2 * peer + row
+                at = slice(g * 8, (g + 1) * 8)
+                columns.append((maxima[r][at], totals[r][at], scales[g][r * 8 : (r + 1) * 8]))
+        out_ref[peer, rows : rows + 16, :] = stat_tile(columns, LENDER_UNIT)
+
+
+LENDER_UNIT = 8.0
+OWNER_UNIT = 1.0
+
+
+def stat_tile(columns, unit):
+    tiles = len(columns)
+    lane = lax.broadcasted_iota(jnp.int32, (8, HEAD_SIZE), 1)
+    top = jnp.zeros((8, HEAD_SIZE), f32)
+    total = top
+    scale = top
+    for c, (m, l, k) in enumerate(columns):
+        top = jnp.where(lane == c, m, top)
+        total = jnp.where((lane == tiles + c) | (lane == 2 * tiles + c), l, total)
+        scale = jnp.where(lane == 3 * tiles + c, k, scale)
+    total = total * unit
+    whole = jnp.floor(total)
+    part = jnp.round((total - whole) * PART)
+    tile = jnp.where(lane < tiles, top, jnp.where(lane < 2 * tiles, whole, part))
+    tile = jnp.where(lane < 3 * tiles, tile, scale)
+    tile = tile.astype(jnp.int32)
+    return jnp.concatenate([tile, jnp.zeros_like(tile)], axis=0).astype(jnp.int16)
+
+
+def merge(parts_ref, groups, unit):
     tiles = 2 * groups
     count = parts_ref.shape[0]
-    stats = [parts_ref[i, tiles * 8 : tiles * 8 + 8, :] for i in range(count)]
+    stats = [
+        parts_ref[i, tiles * 8 : tiles * 8 + 16, :].astype(jnp.int32).astype(f32)[0:8]
+        for i in range(count)
+    ]
     top = stats[0]
     for s in stats[1:]:
         top = jnp.maximum(top, s)
-    scales = [jnp.exp(s - top) for s in stats]
     total = jnp.zeros_like(top)
-    for s, e in zip(stats, scales):
-        total = total + pltpu.roll(s, HEAD_SIZE - tiles, axis=1) * e
+    scales = []
+    for s in stats:
+        shifted = [pltpu.roll(s, HEAD_SIZE - n * tiles, axis=1) for n in (1, 2, 3)]
+        e = jnp.exp(s - top)
+        total = total + (shifted[0] + shifted[1] * (1.0 / PART)) * e
+        scales.append(e * (jnp.exp2(shifted[2] * (1.0 / STEPS)) * (1.0 / FULL)))
     sums = []
-    for c in range(tiles):
-        acc = jnp.zeros((8, HEAD_SIZE), f32)
+    for g in range(groups):
+        pair = [jnp.zeros((8, HEAD_SIZE), f32)] * 2
         for i in range(count):
-            acc = acc + parts_ref[i, c * 8 : (c + 1) * 8, :] * scales[i][:, c : c + 1]
-        sums.append(acc)
-    return top, total, sums
+            both = parts_ref[i, g * 16 : (g + 1) * 16, :].astype(jnp.int32).astype(f32)
+            pair = [
+                pair[n] + both[n * 8 : (n + 1) * 8] * scales[i][:, g * 2 + n : g * 2 + n + 1]
+                for n in range(2)
+            ]
+        sums += pair
+    return top, total * (1.0 / unit), sums
 
 
 def combine_kernel(groups, parts_ref, out_ref):
     tiles = 2 * groups
-    top, total, sums = merge(parts_ref, groups)
-    lane = lax.broadcasted_iota(jnp.int32, (8, HEAD_SIZE), 1)
-    stat = jnp.where(lane < tiles, top, pltpu.roll(total, tiles, axis=1))
+    top, total, sums = merge(parts_ref, groups, LENDER_UNIT)
+    coded = [encode_rows(jnp.concatenate(sums[2 * g : 2 * g + 2], axis=0)) for g in range(groups)]
+    columns = [
+        (top[:, c : c + 1], total[:, c : c + 1], coded[c // 2][0][c % 2 * 8 : c % 2 * 8 + 8])
+        for c in range(tiles)
+    ]
+    stat = stat_tile(columns, OWNER_UNIT)
     for i in range(out_ref.shape[0]):
-        for c in range(tiles):
-            out_ref[i, c * 8 : (c + 1) * 8, :] = sums[c]
-        out_ref[i, tiles * 8 : tiles * 8 + 8, :] = stat
+        for g in range(groups):
+            out_ref[i, g * 16 : (g + 1) * 16, :] = coded[g][1]
+        out_ref[i, tiles * 8 : tiles * 8 + 16, :] = stat
 
 
 def finish_kernel(groups, parts_ref, queries_ref, fresh_ref, out_ref):
-    top, total, sums = merge(parts_ref, groups)
+    top, total, sums = merge(parts_ref, groups, OWNER_UNIT)
     fresh_k = fresh_ref[0].astype(f32)
     fresh_v = fresh_ref[1].astype(f32)
     sub = lax.broadcasted_iota(jnp.int32, (8, HEAD_SIZE), 0)
@@ -269,7 +321,6 @@
         out_shape=jax.ShapeDtypeStruct((lenders, rows + 16, HEAD_SIZE), bf16),
         in_specs=[pl.BlockSpec(memory_space=SMEM)] * 2 + vmem_specs(2),
         out_specs=pl.BlockSpec(memory_space=VMEM),
-        compiler_params=pltpu.CompilerParams(vmem_limit_bytes=16 * 2**20),
         name="send",
     )(page_index, lengths, queries, block_table)
     received = lax.all_to_all(to_send, "inst", 0, 0)
@@ -286,7 +337,7 @@
 
     partial = pl.pallas_call(
         attend_kernel,
-        out_shape=jax.ShapeDtypeStruct((lenders, rows + 8, HEAD_SIZE), f32),
+        out_shape=jax.ShapeDtypeStruct((lenders, rows + 16, HEAD_SIZE), jnp.int16),
         in_specs=vmem_specs(1) + [pl.BlockSpec(memory_space=pltpu.MemorySpace.HBM)],
         out_specs=pl.BlockSpec(memory_space=VMEM),
         scratch_shapes=[
@@ -302,7 +353,7 @@
 
     combined = pl.pallas_call(
         functools.partial(combine_kernel, groups),
-        out_shape=jax.ShapeDtypeStruct((pages, rows + 8, HEAD_SIZE), f32),
+        out_shape=jax.ShapeDtypeStruct((pages, rows + 16, HEAD_SIZE), jnp.int16),
         in_specs=vmem_specs(1),
         out_specs=pl.BlockSpec(memory_space=VMEM),
         compiler_params=pltpu.CompilerParams(vmem_limit_bytes=16 * 2**20),

time: 60.5 us -> 54.5 us (0.901)
  blocking collectives: 34.4 us -> 29.9 us
  local copies, waits for them, and re-layouts: 2.07 us -> 0.01 us
  Pallas kernels: 14.1 us -> 14.8 us
    all_to_all x1, blocking collectives: 15.3 us -> 12.3 us  [shards(): parts = lax.all_to_all(partial, 'inst', 0, 0)]
    unnamed x10 -> x4, local copies, waits for them, and re-layouts: 2.07 us -> 0.01 us
    all_to_all x1, blocking collectives: 19.1 us -> 17.7 us  [shards(): page_parts = lax.all_to_all(combined, 'page', 0, 0)]
  transfers between devices with their start and end apart: 1 -> 1, of which waited for: 1 -> 1; matrix products, arithmetic and copies ran while one was open for 0% -> 0% of each run, Pallas kernels for 9% -> 10%
where the time goes in v3:
time: 54.5 us; the launch traced here: 54.2 us
  blocking collectives  29.9 us (55%)
  Pallas kernels  14.8 us (27%)
  starting transfers between devices  7.39 us (14%)
  waiting for transfers between devices  2.05 us (4%)
    all_to_all x1, blocking collectives, shards(): page_parts = lax.all_to_all(combined, 'page', 0, 0)  17.7 us
    all_to_all x1, blocking collectives, shards(): parts = lax.all_to_all(partial, 'inst', 0, 0)  12.3 us
    all_to_all x1, starting transfers between devices, shards(): received = lax.all_to_all(to_send, 'inst', 0, 0)  7.39 us
    pallas_call x1, Pallas kernels, shards(): pl.pallas_call(attend_kernel, out_shape=jax.ShapeDtypeStruct((lenders, ro...  5.72 us
    pallas_call x1, Pallas kernels, shards(): pl.pallas_call(token_major_kernel, grid=(2, 2), out_shape=jax.ShapeDtypeS...  5.6 us
    all_to_all x1, waiting for transfers between devices, shards(): received = lax.all_to_all(to_send, 'inst', 0, 0)  2.05 us
    pallas_call x1, Pallas kernels, shards(): pl.pallas_call(functools.partial(send_kernel, slots, pages), out_shape=ja...  1.74 us
    pallas_call x1, Pallas kernels, shards(): pl.pallas_call(functools.partial(finish_kernel, groups), out_shape=jax.Sh...  1.25 us
  transfers between devices with their start and end apart: 1, of which 1 were waited for; matrix products, arithmetic and copies ran while one was open for 0% of the time, Pallas kernels for 10%

profile of v3, /device:TPU:8, one launch (start us, length us, event | category | flops | bytes accessed | tf_op | source)
XLA Modules:
  0.0 54.2 jit_solution(9408388445470777599)
XLA Ops:
  0.0 1.7 %send.1 = bf16[16,80,128]{2,1,0:T(8,128)(2,1)} custom-call(s32[1]{0:T(128)} %bitcast.page_ref, s32[2]{0:T(128)} %lengths_ref.1, bf16[2,4096]{1,0:T(2,128)(2,1)} %queries_ref.3, s32[2,768]{1,0:T(2,128)} %table_ref.1), custom_call_target="tpu_custom_call" | custom-call | tf_op jit(solution)/shard_map/send/pallas_call | solution.py:319
  1.7 7.4 %all-to-all-start = ((bf16[16,80,128]{2,1,0:T(8,128)(2,1)}), bf16[16,80,128]{2,1,0:T(8,128)(2,1)S(1)}, u32[]{:S(2)}, u32[]{:S(2)}) async-start(bf16[16,80,128]{2,1,0:T(8,128)(2,1)} %send.1), calls=%async_computation | async-start | bytes 655360 | tf_op jit(solution)/shard_map/all_to_all | solution.py:326
  9.1 5.6 %token_major.1.kv_hbm = bf16[2,16,128,512]{3,2,1,0:T(8,128)(2,1)} custom-call(bf16[2,128,16,512]{3,2,1,0:T(8,128)(2,1)} %pool_ref.1), custom_call_target="tpu_custom_call" | custom-call | flops 1000000000 | bytes 8388608 | tf_op jit(solution)/shard_map/token_major/pallas_call | solution.py:328
  14.7 0.0 copy-start
  14.7 0.0 copy-start.1
  14.7 2.1 %all-to-all-done.recv_ref = bf16[16,80,128]{2,1,0:T(8,128)(2,1)S(1)} async-done(((bf16[16,80,128]{2,1,0:T(8,128)(2,1)}), bf16[16,80,128]{2,1,0:T(8,128)(2,1)S(1)}, u32[]{:S(2)}, u32[]{:S(2)}) %all-to-all-start) | async-done | bytes 327712 | tf_op jit(solution)/shard_map/all_to_all | solution.py:326
  16.8 5.7 %attend.1 = s16[16,80,128]{2,1,0:T(8,128)(2,1)S(1)} custom-call(bf16[16,80,128]{2,1,0:T(8,128)(2,1)S(1)} %all-to-all-done.recv_ref, bf16[2,16,128,512]{3,2,1,0:T(8,128)(2,1)} %token_major.1.kv_hbm), custom_call_target="tpu_custom_call" | custom-call | tf_op jit(solution)/shard_map/attend/pallas_call | solution.py:338
  22.5 12.3 %all_to_all.15.parts_ref = s16[16,80,128]{2,1,0:T(8,128)(2,1)S(1)} all-to-all(s16[16,80,128]{2,1,0:T(8,128)(2,1)S(1)} %attend.1), channel_id=1, replica_groups=mesh['inst'=16,'page'=8,'head'=2] {'inst'}, dimensions={0} | all-to-all | bytes 655360 | tf_op jit(solution)/shard_map/all_to_all | solution.py:352
  34.8 0.5 combine.1
  35.2 17.7 %all_to_all.16.parts_ref = s16[8,80,128]{2,1,0:T(8,128)(2,1)S(1)} all-to-all(s16[8,80,128]{2,1,0:T(8,128)(2,1)S(1)} %combine.1), channel_id=1, replica_groups=mesh['inst'=16,'page'=8,'head'=2] {'page'}, dimensions={0} | all-to-all | bytes 327680 | tf_op jit(solution)/shard_map/all_to_all | solution.py:362
  52.9 0.0 copy-done
  52.9 0.0 copy-done.1
  52.9 1.2 %finish.1 = bf16[2,4096]{1,0:T(2,128)(2,1)} custom-call(s16[8,80,128]{2,1,0:T(8,128)(2,1)S(1)} %all_to_all.16.parts_ref, bf16[2,4096]{1,0:T(2,128)(2,1)S(1)} %copy-done, bf16[2,2,512]{2,1,0:T(2,128)(2,1)S(1)} %copy-done.1), custom_call_target="tpu_custom_call" | custom-call | tf_op jit(solution)/shard_map/finish/pallas_call | solution.py:364
Async XLA Ops:
  1.7 15.0 %all-to-all-start = ((bf16[16,80,128]{2,1,0:T(8,128)(2,1)}), bf16[16,80,128]{2,1,0:T(8,128)(2,1)S(1)}, u32[]{:S(2)}, u32[]{:S(2)}) async-start(bf16[16,80,128]{2,1,0:T(8,128)(2,1)} %send.1), calls=%async_computation | async-start | bytes 655360 | tf_op jit(solution)/shard_map/all_to_all | solution.py:326
  14.7 38.2 %copy-start = (bf16[2,4096]{1,0:T(2,128)(2,1)S(1)}, bf16[2,4096]{1,0:T(2,128)(2,1)}, u32[]{:S(2)}) copy-start(bf16[2,4096]{1,0:T(2,128)(2,1)} %queries_ref.3) | copy-start | bytes 49156
  14.7 38.2 %copy-start.1 = (bf16[2,2,512]{2,1,0:T(2,128)(2,1)S(1)}, bf16[2,2,512]{2,1,0:T(2,128)(2,1)}, u32[]{:S(2)}) copy-start(bf16[2,2,512]{2,1,0:T(2,128)(2,1)} %fresh_ref.1) | copy-start | bytes 12292

commit v4 on v3

--- a/solution.py
+++ b/solution.py
@@ -80,16 +80,44 @@
         out_ref[peer, rows : rows + 16, :] = tile.astype(bf16)
 
 
-def token_major_kernel(pool_ref, out_ref):
-    pages, page_tok, width = pool_ref.shape[1:]
+PARTS = 2
+
+
+def token_major_kernel(pool_hbm, out_hbm, pool_ref, out_ref, load_sems, store_sems):
+    pages, page_tok, width = pool_hbm.shape[1:]
+    chunk = pages // PARTS
     block = page_tok * 16
+    loads = []
+    stores = []
+    for kind in range(2):
+        for c in range(PARTS):
+            at = pl.ds(c * chunk, chunk)
+            loads.append(
+                pltpu.make_async_copy(
+                    pool_hbm.at[kind, at], pool_ref.at[kind, at], load_sems.at[kind, c]
+                )
+            )
+            stores.append(
+                pltpu.make_async_copy(
+                    out_ref.at[kind, :, at], out_hbm.at[kind, :, at], store_sems.at[kind, c]
+                )
+            )
+    for load in loads:
+        load.start()
     i = lax.broadcasted_iota(jnp.int32, (block, block), 0)
     j = lax.broadcasted_iota(jnp.int32, (block, block), 1)
     perm = jnp.where((i % 16) * page_tok + i // 16 == j, 1.0, 0.0).astype(bf16)
-    for b in range(pages // 16):
-        rows = pool_ref[0, b * 16 : (b + 1) * 16].reshape(block, width)
-        moved = jnp.dot(perm, rows, preferred_element_type=f32).astype(bf16)
-        out_ref[0, :, b * 16 : (b + 1) * 16, :] = moved.reshape(page_tok, 16, width)
+    for kind in range(2):
+        for c in range(PARTS):
+            loads[kind * PARTS + c].wait()
+            for b in range(chunk // 16):
+                first = c * chunk + b * 16
+                rows = pool_ref[kind, first : first + 16].reshape(block, width)
+                moved = jnp.dot(perm, rows, preferred_element_type=f32).astype(bf16)
+                out_ref[kind, :, first : first + 16, :] = moved.reshape(page_tok, 16, width)
+            stores[kind * PARTS + c].start()
+    for store in stores:
+        store.wait()
 
 
 CHUNKS = 4
@@ -327,10 +355,15 @@
 
     kv = pl.pallas_call(
         token_major_kernel,
-        grid=(2, 2),
         out_shape=jax.ShapeDtypeStruct((2, page_tok, slots, width), bf16),
-        in_specs=[pl.BlockSpec((1, slots // 2, page_tok, width), lambda i, j: (i, j, 0, 0))],
-        out_specs=pl.BlockSpec((1, page_tok, slots // 2, width), lambda i, j: (i, 0, j, 0)),
+        in_specs=[pl.BlockSpec(memory_space=pl.ANY)],
+        out_specs=pl.BlockSpec(memory_space=pl.ANY),
+        scratch_shapes=[
+            pltpu.VMEM(key_value_pool.shape, bf16),
+            pltpu.VMEM((2, page_tok, slots, width), bf16),
+            pltpu.SemaphoreType.DMA((2, PARTS)),
+            pltpu.SemaphoreType.DMA((2, PARTS)),
+        ],
         cost_estimate=pl.CostEstimate(flops=10**9, bytes_accessed=2 * 4 * 2**20, transcendentals=0),
         name="token_major",
     )(key_value_pool)

time: 54.5 us -> 54.5 us (level)
  Pallas kernels: 14.8 us -> 13.2 us
  waiting for transfers between devices: 2.05 us -> 3.54 us
    pallas_call x1, Pallas kernels: 5.6 us -> 4.08 us  [shards(): pl.pallas_call(token_major_kernel, out_shape=jax.ShapeDtypeStruct((2, pag...]
    all_to_all x1, waiting for transfers between devices: 2.05 us -> 3.54 us  [shards(): received = lax.all_to_all(to_send, 'inst', 0, 0)]
  transfers between devices with their start and end apart: 1 -> 1, of which waited for: 1 -> 1; matrix products, arithmetic and copies ran while one was open for 0% -> 0% of each run, Pallas kernels for 10% -> 8%
where the time goes in v4:
time: 54.5 us; the launch traced here: 54.2 us
  blocking collectives  30 us (55%)
  Pallas kernels  13.2 us (24%)
  starting transfers between devices  7.39 us (14%)
  waiting for transfers between devices  3.54 us (6%)
    all_to_all x1, blocking collectives, shards(): page_parts = lax.all_to_all(combined, 'page', 0, 0)  17.7 us
    all_to_all x1, blocking collectives, shards(): parts = lax.all_to_all(partial, 'inst', 0, 0)  12.3 us
    all_to_all x1, starting transfers between devices, shards(): received = lax.all_to_all(to_send, 'inst', 0, 0)  7.39 us
    pallas_call x1, Pallas kernels, shards(): pl.pallas_call(attend_kernel, out_shape=jax.ShapeDtypeStruct((lenders, ro...  5.72 us
    pallas_call x1, Pallas kernels, shards(): pl.pallas_call(token_major_kernel, out_shape=jax.ShapeDtypeStruct((2, pag...  4.08 us
    all_to_all x1, waiting for transfers between devices, shards(): received = lax.all_to_all(to_send, 'inst', 0, 0)  3.54 us
    pallas_call x1, Pallas kernels, shards(): pl.pallas_call(functools.partial(send_kernel, slots, pages), out_shape=ja...  1.74 us
    pallas_call x1, Pallas kernels, shards(): pl.pallas_call(functools.partial(finish_kernel, groups), out_shape=jax.Sh...  1.25 us
  transfers between devices with their start and end apart: 1, of which 1 were waited for; matrix products, arithmetic and copies ran while one was open for 0% of the time, Pallas kernels for 8%

profile of v4, /device:TPU:8, one launch (start us, length us, event | category | flops | bytes accessed | tf_op | source)
XLA Modules:
  0.0 54.2 jit_solution(1618284404308036075)
XLA Ops:
  0.0 1.7 %send.1 = bf16[16,80,128]{2,1,0:T(8,128)(2,1)} custom-call(s32[1]{0:T(128)} %bitcast.page_ref, s32[2]{0:T(128)} %lengths_ref.1, bf16[2,4096]{1,0:T(2,128)(2,1)} %queries_ref.3, s32[2,768]{1,0:T(2,128)} %table_ref.1), custom_call_target="tpu_custom_call" | custom-call | tf_op jit(solution)/shard_map/send/pallas_call | solution.py:347
  1.7 7.4 %all-to-all-start = ((bf16[16,80,128]{2,1,0:T(8,128)(2,1)}), bf16[16,80,128]{2,1,0:T(8,128)(2,1)S(1)}, u32[]{:S(2)}, u32[]{:S(2)}) async-start(bf16[16,80,128]{2,1,0:T(8,128)(2,1)} %send.1), calls=%async_computation | async-start | bytes 655360 | tf_op jit(solution)/shard_map/all_to_all | solution.py:354
  9.1 4.1 %token_major.1.kv_hbm = bf16[2,16,128,512]{3,2,1,0:T(8,128)(2,1)} custom-call(bf16[2,128,16,512]{3,2,1,0:T(8,128)(2,1)} %pool_hbm.1), custom_call_target="tpu_custom_call" | custom-call | flops 1000000000 | bytes 8388608 | tf_op jit(solution)/shard_map/token_major/pallas_call | solution.py:356
  13.2 0.0 copy-start
  13.2 0.0 copy-start.1
  13.2 3.5 %all-to-all-done.recv_ref = bf16[16,80,128]{2,1,0:T(8,128)(2,1)S(1)} async-done(((bf16[16,80,128]{2,1,0:T(8,128)(2,1)}), bf16[16,80,128]{2,1,0:T(8,128)(2,1)S(1)}, u32[]{:S(2)}, u32[]{:S(2)}) %all-to-all-start) | async-done | bytes 327712 | tf_op jit(solution)/shard_map/all_to_all | solution.py:354
  16.8 5.7 %attend.1 = s16[16,80,128]{2,1,0:T(8,128)(2,1)S(1)} custom-call(bf16[16,80,128]{2,1,0:T(8,128)(2,1)S(1)} %all-to-all-done.recv_ref, bf16[2,16,128,512]{3,2,1,0:T(8,128)(2,1)} %token_major.1.kv_hbm), custom_call_target="tpu_custom_call" | custom-call | tf_op jit(solution)/shard_map/attend/pallas_call | solution.py:371
  22.5 12.3 %all_to_all.15.parts_ref = s16[16,80,128]{2,1,0:T(8,128)(2,1)S(1)} all-to-all(s16[16,80,128]{2,1,0:T(8,128)(2,1)S(1)} %attend.1), channel_id=1, replica_groups=mesh['inst'=16,'page'=8,'head'=2] {'inst'}, dimensions={0} | all-to-all | bytes 655360 | tf_op jit(solution)/shard_map/all_to_all | solution.py:385
  34.8 0.5 combine.1
  35.3 17.7 %all_to_all.16.parts_ref = s16[8,80,128]{2,1,0:T(8,128)(2,1)S(1)} all-to-all(s16[8,80,128]{2,1,0:T(8,128)(2,1)S(1)} %combine.1), channel_id=1, replica_groups=mesh['inst'=16,'page'=8,'head'=2] {'page'}, dimensions={0} | all-to-all | bytes 327680 | tf_op jit(solution)/shard_map/all_to_all | solution.py:395
  53.0 0.0 copy-done
  53.0 0.0 copy-done.1
  53.0 1.2 %finish.1 = bf16[2,4096]{1,0:T(2,128)(2,1)} custom-call(s16[8,80,128]{2,1,0:T(8,128)(2,1)S(1)} %all_to_all.16.parts_ref, bf16[2,4096]{1,0:T(2,128)(2,1)S(1)} %copy-done, bf16[2,2,512]{2,1,0:T(2,128)(2,1)S(1)} %copy-done.1), custom_call_target="tpu_custom_call" | custom-call | tf_op jit(solution)/shard_map/finish/pallas_call | solution.py:397
Async XLA Ops:
  1.7 15.0 %all-to-all-start = ((bf16[16,80,128]{2,1,0:T(8,128)(2,1)}), bf16[16,80,128]{2,1,0:T(8,128)(2,1)S(1)}, u32[]{:S(2)}, u32[]{:S(2)}) async-start(bf16[16,80,128]{2,1,0:T(8,128)(2,1)} %send.1), calls=%async_computation | async-start | bytes 655360 | tf_op jit(solution)/shard_map/all_to_all | solution.py:354
  13.2 39.8 %copy-start = (bf16[2,4096]{1,0:T(2,128)(2,1)S(1)}, bf16[2,4096]{1,0:T(2,128)(2,1)}, u32[]{:S(2)}) copy-start(bf16[2,4096]{1,0:T(2,128)(2,1)} %queries_ref.3) | copy-start | bytes 49156
  13.2 39.7 %copy-start.1 = (bf16[2,2,512]{2,1,0:T(2,128)(2,1)S(1)}, bf16[2,2,512]{2,1,0:T(2,128)(2,1)}, u32[]{:S(2)}) copy-start(bf16[2,2,512]{2,1,0:T(2,128)(2,1)} %fresh_ref.1) | copy-start | bytes 12292

commit v5 on v4

--- a/solution.py
+++ b/solution.py
@@ -303,31 +303,47 @@
         out_ref[i, tiles * 8 : tiles * 8 + 16, :] = stat
 
 
-def finish_kernel(groups, parts_ref, queries_ref, fresh_ref, out_ref):
-    top, total, sums = merge(parts_ref, groups, OWNER_UNIT)
+def new_token_kernel(groups, queries_ref, fresh_ref, out_ref):
+    sub = lax.broadcasted_iota(jnp.int32, (8, HEAD_SIZE), 0)
+    lane = lax.broadcasted_iota(jnp.int32, (8, HEAD_SIZE), 1)
     fresh_k = fresh_ref[0].astype(f32)
     fresh_v = fresh_ref[1].astype(f32)
-    sub = lax.broadcasted_iota(jnp.int32, (8, HEAD_SIZE), 0)
+    values = jnp.zeros((8, HEAD_SIZE), f32)
+    tile = jnp.zeros((8, HEAD_SIZE), f32)
     for g in range(groups):
         both = [
             queries_ref[:, (g * 8 + h) * HEAD_SIZE : (g * 8 + h + 1) * HEAD_SIZE].astype(f32)
             for h in range(8)
         ]
-        outs = []
         for row in range(2):
-            c = g * 2 + row
             q = jnp.zeros((8, HEAD_SIZE), f32)
             for h in range(8):
                 q = jnp.where(sub == h, both[h][row : row + 1, :], q)
             k = fresh_k[row : row + 1, g * HEAD_SIZE : (g + 1) * HEAD_SIZE]
+            new = jnp.sum(q * k, axis=1, keepdims=True) * SCALE
+            tile = jnp.where(lane == g * 2 + row, new, tile)
             v = fresh_v[row : row + 1, g * HEAD_SIZE : (g + 1) * HEAD_SIZE]
-            new = jnp.sum(q * k, axis=1, keepdims=True) * SCALE
-            cache = top[:, c : c + 1]
-            best = jnp.maximum(cache, new)
-            carried = jnp.exp(cache - best)
-            own = jnp.exp(new - best)
-            denominator = own + total[:, c : c + 1] * carried
-            outs.append((own * v + sums[c] * carried) / denominator)
+            values = jnp.where(sub == g * 2 + row, v, values)
+    out_ref[0:8, :] = tile
+    out_ref[8:16, :] = values
+
+
+def finish_kernel(groups, parts_ref, token_ref, out_ref):
+    top, total, sums = merge(parts_ref, groups, OWNER_UNIT)
+    new = token_ref[0:8, :]
+    best = jnp.maximum(top, new)
+    carried = jnp.exp(top - best)
+    own = jnp.exp(new - best)
+    denominator = own + total * carried
+    for g in range(groups):
+        outs = []
+        for row in range(2):
+            c = g * 2 + row
+            at = slice(c, c + 1)
+            outs.append(
+                (own[:, at] * token_ref[8 + c : 9 + c, :] + sums[c] * carried[:, at])
+                / denominator[:, at]
+            )
         for h in range(8):
             at = (g * 8 + h) * HEAD_SIZE
             out_ref[:, at : at + HEAD_SIZE] = jnp.concatenate(
@@ -392,16 +408,27 @@
         compiler_params=pltpu.CompilerParams(vmem_limit_bytes=16 * 2**20),
         name="combine",
     )(parts)
+    combined, last_queries, last_fresh = lax.optimization_barrier(
+        (combined, queries, fresh_key_value)
+    )
     page_parts = lax.all_to_all(combined, "page", 0, 0)
+    token = pl.pallas_call(
+        functools.partial(new_token_kernel, groups),
+        out_shape=jax.ShapeDtypeStruct((16, HEAD_SIZE), f32),
+        in_specs=vmem_specs(2),
+        out_specs=pl.BlockSpec(memory_space=VMEM),
+        cost_estimate=pl.CostEstimate(flops=10**6, bytes_accessed=2**16, transcendentals=0),
+        name="new_token",
+    )(last_queries, last_fresh)
 
     return pl.pallas_call(
         functools.partial(finish_kernel, groups),
         out_shape=jax.ShapeDtypeStruct(queries.shape, bf16),
-        in_specs=vmem_specs(3),
+        in_specs=vmem_specs(2),
         out_specs=pl.BlockSpec(memory_space=VMEM),
         compiler_params=pltpu.CompilerParams(vmem_limit_bytes=16 * 2**20),
         name="finish",
-    )(page_parts, queries, fresh_key_value)
+    )(page_parts, token)
 
 
 def solution(mesh):

time: 54.5 us -> 55.8 us (1.024)
  blocking collectives: 30 us -> 12.3 us
  starting transfers between devices: 7.39 us -> 15.9 us
  waiting for transfers between devices: 3.54 us -> 11.6 us
  Pallas kernels: 13.2 us -> 14.9 us
  local copies, waits for them, and re-layouts: 0.01 us -> 0.7 us
    all_to_all x1 -> x0, blocking collectives: 17.7 us -> none  [shards(): page_parts = lax.all_to_all(combined, 'page', 0, 0)]
    all_to_all x0 -> x1, starting transfers between devices: none -> 8.46 us  [shards(): page_parts = lax.all_to_all(combined, 'page', 0, 0)]
    all_to_all x0 -> x1, waiting for transfers between devices: none -> 8.01 us  [shards(): page_parts = lax.all_to_all(combined, 'page', 0, 0)]
    pallas_call x0 -> x1, Pallas kernels: none -> 1.42 us  [shards(): pl.pallas_call(functools.partial(new_token_kernel, groups), out_shape=jax...]
    unnamed x4 -> x2, local copies, waits for them, and re-layouts: 0.01 us -> 0.7 us
    pallas_call x1, Pallas kernels: 0.47 us -> 1.13 us  [shards(): pl.pallas_call(functools.partial(combine_kernel, groups), out_shape=jax.S...]
  transfers between devices with their start and end apart: 1 -> 2, of which waited for: 1 -> 2; matrix products, arithmetic and copies ran while one was open for 0% -> 0% of each run, Pallas kernels for 8% -> 10%
where the time goes in v5:
time: 55.8 us; the launch traced here: 55.4 us
  starting transfers between devices  15.9 us (28%)
  Pallas kernels  14.9 us (27%)
  blocking collectives  12.3 us (22%)
  waiting for transfers between devices  11.6 us (21%)
  local copies, waits for them, and re-layouts  0.7 us (1%)
    all_to_all x1, blocking collectives, shards(): parts = lax.all_to_all(partial, 'inst', 0, 0)  12.3 us
    all_to_all x1, starting transfers between devices, shards(): page_parts = lax.all_to_all(combined, 'page', 0, 0)  8.46 us
    all_to_all x1, waiting for transfers between devices, shards(): page_parts = lax.all_to_all(combined, 'page', 0, 0)  8.01 us
    all_to_all x1, starting transfers between devices, shards(): received = lax.all_to_all(to_send, 'inst', 0, 0)  7.39 us
    pallas_call x1, Pallas kernels, shards(): pl.pallas_call(attend_kernel, out_shape=jax.ShapeDtypeStruct((lenders, ro...  5.7 us
    pallas_call x1, Pallas kernels, shards(): pl.pallas_call(token_major_kernel, out_shape=jax.ShapeDtypeStruct((2, pag...  4.02 us
    all_to_all x1, waiting for transfers between devices, shards(): received = lax.all_to_all(to_send, 'inst', 0, 0)  3.63 us
    pallas_call x1, Pallas kernels, shards(): pl.pallas_call(functools.partial(send_kernel, slots, pages), out_shape=ja...  1.74 us
  transfers between devices with their start and end apart: 2, of which 2 were waited for; matrix products, arithmetic and copies ran while one was open for 0% of the time, Pallas kernels for 10%

profile of v5, /device:TPU:8, one launch (start us, length us, event | category | flops | bytes accessed | tf_op | source)
XLA Modules:
  0.0 55.4 jit_solution(18214109347791896035)
XLA Ops:
  0.0 1.7 %send.1 = bf16[16,80,128]{2,1,0:T(8,128)(2,1)} custom-call(s32[1]{0:T(128)} %bitcast.page_ref, s32[2]{0:T(128)} %lengths_ref.1, bf16[2,4096]{1,0:T(2,128)(2,1)} %queries_ref.2, s32[2,768]{1,0:T(2,128)} %table_ref.1), custom_call_target="tpu_custom_call" | custom-call | tf_op jit(solution)/shard_map/send/pallas_call | solution.py:363
  1.7 7.4 %all-to-all-start = ((bf16[16,80,128]{2,1,0:T(8,128)(2,1)}), bf16[16,80,128]{2,1,0:T(8,128)(2,1)S(1)}, u32[]{:S(2)}, u32[]{:S(2)}) async-start(bf16[16,80,128]{2,1,0:T(8,128)(2,1)} %send.1), calls=%async_computation | async-start | bytes 655360 | tf_op jit(solution)/shard_map/all_to_all | solution.py:370
  9.1 4.0 %token_major.1.kv_hbm = bf16[2,16,128,512]{3,2,1,0:T(8,128)(2,1)} custom-call(bf16[2,128,16,512]{3,2,1,0:T(8,128)(2,1)} %pool_hbm.1), custom_call_target="tpu_custom_call" | custom-call | flops 1000000000 | bytes 8388608 | tf_op jit(solution)/shard_map/token_major/pallas_call | solution.py:372
  13.2 3.6 %all-to-all-done.recv_ref = bf16[16,80,128]{2,1,0:T(8,128)(2,1)S(1)} async-done(((bf16[16,80,128]{2,1,0:T(8,128)(2,1)}), bf16[16,80,128]{2,1,0:T(8,128)(2,1)S(1)}, u32[]{:S(2)}, u32[]{:S(2)}) %all-to-all-start) | async-done | bytes 327712 | tf_op jit(solution)/shard_map/all_to_all | solution.py:370
  16.8 5.7 %attend.1 = s16[16,80,128]{2,1,0:T(8,128)(2,1)S(1)} custom-call(bf16[16,80,128]{2,1,0:T(8,128)(2,1)S(1)} %all-to-all-done.recv_ref, bf16[2,16,128,512]{3,2,1,0:T(8,128)(2,1)} %token_major.1.kv_hbm), custom_call_target="tpu_custom_call" | custom-call | tf_op jit(solution)/shard_map/attend/pallas_call | solution.py:387
  22.5 12.3 %all_to_all.15.parts_ref = s16[16,80,128]{2,1,0:T(8,128)(2,1)S(1)} all-to-all(s16[16,80,128]{2,1,0:T(8,128)(2,1)S(1)} %attend.1), channel_id=1, replica_groups=mesh['inst'=16,'page'=8,'head'=2] {'inst'}, dimensions={0} | all-to-all | bytes 655360 | tf_op jit(solution)/shard_map/all_to_all | solution.py:401
  34.8 1.1 %combine.1 = s16[8,80,128]{2,1,0:T(8,128)(2,1)} custom-call(s16[16,80,128]{2,1,0:T(8,128)(2,1)S(1)} %all_to_all.15.parts_ref), custom_call_target="tpu_custom_call" | custom-call | tf_op jit(solution)/shard_map/combine/pallas_call | solution.py:403
  35.9 8.5 %all-to-all-start.2 = ((s16[8,80,128]{2,1,0:T(8,128)(2,1)}), s16[8,80,128]{2,1,0:T(8,128)(2,1)S(1)}, u32[]{:S(2)}, u32[]{:S(2)}) async-start(s16[8,80,128]{2,1,0:T(8,128)(2,1)} %combine.1), calls=%async_computation.2 | async-start | bytes 327680 | tf_op jit(solution)/shard_map/all_to_all | solution.py:414
  44.4 1.4 %new_token.1.token_ref = f32[16,128]{1,0:T(8,128)} custom-call(bf16[2,4096]{1,0:T(2,128)(2,1)} %queries_ref.2, bf16[2,2,512]{2,1,0:T(2,128)(2,1)} %fresh_ref), custom_call_target="tpu_custom_call" | custom-call | flops 1000000 | bytes 65536 | tf_op jit(solution)/shard_map/new_token/pallas_call | solution.py:415
  45.8 8.0 %all-to-all-done.2.parts_ref = s16[8,80,128]{2,1,0:T(8,128)(2,1)S(1)} async-done(((s16[8,80,128]{2,1,0:T(8,128)(2,1)}), s16[8,80,128]{2,1,0:T(8,128)(2,1)S(1)}, u32[]{:S(2)}, u32[]{:S(2)}) %all-to-all-start.2) | async-done | bytes 163872 | tf_op jit(solution)/shard_map/all_to_all | solution.py:414
  53.8 0.0 copy-start
  53.8 0.7 %copy-done = f32[16,128]{1,0:T(8,128)S(1)} copy-done((f32[16,128]{1,0:T(8,128)S(1)}, f32[16,128]{1,0:T(8,128)}, u32[]{:S(2)}) %copy-start) | copy-done | bytes 8216
  54.5 0.9 %finish.1 = bf16[2,4096]{1,0:T(2,128)(2,1)} custom-call(s16[8,80,128]{2,1,0:T(8,128)(2,1)S(1)} %all-to-all-done.2.parts_ref, f32[16,128]{1,0:T(8,128)S(1)} %copy-done), custom_call_target="tpu_custom_call" | custom-call | tf_op jit(solution)/shard_map/finish/pallas_call | solution.py:424
Async XLA Ops:
  1.7 15.0 %all-to-all-start = ((bf16[16,80,128]{2,1,0:T(8,128)(2,1)}), bf16[16,80,128]{2,1,0:T(8,128)(2,1)S(1)}, u32[]{:S(2)}, u32[]{:S(2)}) async-start(bf16[16,80,128]{2,1,0:T(8,128)(2,1)} %send.1), calls=%async_computation | async-start | bytes 655360 | tf_op jit(solution)/shard_map/all_to_all | solution.py:370
  35.9 17.9 %all-to-all-start.2 = ((s16[8,80,128]{2,1,0:T(8,128)(2,1)}), s16[8,80,128]{2,1,0:T(8,128)(2,1)S(1)}, u32[]{:S(2)}, u32[]{:S(2)}) async-start(s16[8,80,128]{2,1,0:T(8,128)(2,1)} %combine.1), calls=%async_computation.2 | async-start | bytes 327680 | tf_op jit(solution)/shard_map/all_to_all | solution.py:414
  53.8 0.7 %copy-start = (f32[16,128]{1,0:T(8,128)S(1)}, f32[16,128]{1,0:T(8,128)}, u32[]{:S(2)}) copy-start(f32[16,128]{1,0:T(8,128)} %new_token.1.token_ref) | copy-start | bytes 24580

commit v6 on v5

--- a/solution.py
+++ b/solution.py
@@ -71,19 +71,47 @@
         pieces += pair
     queries = jnp.concatenate(pieces, axis=0).astype(bf16)
     rows = own_rows * heads
-    sub = lax.broadcasted_iota(jnp.int32, (16, slots), 0)
+    sub = lax.broadcasted_iota(jnp.int32, (8, slots), 0)
     for peer in range(peers):
         out_ref[peer, 0:rows, :] = queries
-        tile = jnp.zeros((16, slots), f32)
+        tile = jnp.zeros((8, slots), f32)
         for row in range(own_rows):
             tile = jnp.where(sub == row, fills[row][peer : peer + 1, :], tile)
-        out_ref[peer, rows : rows + 16, :] = tile.astype(bf16)
+        out_ref[peer, rows : rows + 8, :] = tile.astype(bf16)
+
+
+def new_token(queries_ref, fresh_ref, token_ref):
+    groups = fresh_ref.shape[2] // HEAD_SIZE
+    sub = lax.broadcasted_iota(jnp.int32, (8, HEAD_SIZE), 0)
+    lane = lax.broadcasted_iota(jnp.int32, (8, HEAD_SIZE), 1)
+    fresh_k = fresh_ref[0].astype(f32)
+    fresh_v = fresh_ref[1].astype(f32)
+    scores = jnp.zeros((8, HEAD_SIZE), f32)
+    values = jnp.zeros((8, HEAD_SIZE), f32)
+    for g in range(groups):
+        both = [
+            queries_ref[:, (g * 8 + h) * HEAD_SIZE : (g * 8 + h + 1) * HEAD_SIZE].astype(f32)
+            for h in range(8)
+        ]
+        for row in range(2):
+            q = jnp.zeros((8, HEAD_SIZE), f32)
+            for h in range(8):
+                q = jnp.where(sub == h, both[h][row : row + 1, :], q)
+            k = fresh_k[row : row + 1, g * HEAD_SIZE : (g + 1) * HEAD_SIZE]
+            new = jnp.sum(q * k, axis=1, keepdims=True) * SCALE
+            scores = jnp.where(lane == g * 2 + row, new, scores)
+            v = fresh_v[row : row + 1, g * HEAD_SIZE : (g + 1) * HEAD_SIZE]
+            values = jnp.where(sub == g * 2 + row, v, values)
+    token_ref[0:8, :] = scores
+    token_ref[8:16, :] = values
 
 
 PARTS = 2
 
 
-def token_major_kernel(pool_hbm, out_hbm, pool_ref, out_ref, load_sems, store_sems):
+def token_major_kernel(
+    pool_hbm, queries_ref, fresh_ref, out_hbm, token_ref, pool_ref, out_ref, load_sems, store_sems
+):
     pages, page_tok, width = pool_hbm.shape[1:]
     chunk = pages // PARTS
     block = page_tok * 16
@@ -106,6 +134,7 @@
         load.start()
     i = lax.broadcasted_iota(jnp.int32, (block, block), 0)
     j = lax.broadcasted_iota(jnp.int32, (block, block), 1)
+    new_token(queries_ref, fresh_ref, token_ref)
     perm = jnp.where((i % 16) * page_tok + i // 16 == j, 1.0, 0.0).astype(bf16)
     for kind in range(2):
         for c in range(PARTS):
@@ -120,27 +149,27 @@
         store.wait()
 
 
-CHUNKS = 4
+KEY_LOADS = (4, 12)
+VALUE_LOADS = (16,)
+UNROLL = True
 
 
 def attend_kernel(recv_ref, kv_hbm, out_ref, kv_ref, score_ref, weight_ref, sems):
     peers = recv_ref.shape[0]
     page_tok, slots, width = kv_ref.shape[1:]
-    step = page_tok // CHUNKS
-    loads = [
-        [
-            pltpu.make_async_copy(
-                kv_hbm.at[kind, pl.ds(c * step, step)],
-                kv_ref.at[kind, pl.ds(c * step, step)],
-                sems.at[kind, c],
+    loads = []
+    for kind, sizes in enumerate((KEY_LOADS, VALUE_LOADS)):
+        first = 0
+        for size in sizes:
+            at = pl.ds(first, size)
+            copy = pltpu.make_async_copy(
+                kv_hbm.at[kind, at], kv_ref.at[kind, at], sems.at[len(loads)]
             )
-            for c in range(CHUNKS)
-        ]
-        for kind in range(2)
-    ]
-    for kind in range(2):
-        for c in range(CHUNKS):
-            loads[kind][c].start()
+            copy.start()
+            loads.append((first, size, copy))
+            first += size
+    key_loads = loads[: len(KEY_LOADS)]
+    value_loads = loads[len(KEY_LOADS) :]
     groups = width // HEAD_SIZE
     requests = 2 * peers
     heads = groups * 8
@@ -149,7 +178,7 @@
     fill = jnp.zeros((8, slots), f32)
     code = jnp.zeros((8, slots), f32)
     for peer in range(peers):
-        tile = recv_ref[peer, rows : rows + 16, :].astype(f32)[0:8]
+        tile = recv_ref[peer, rows : rows + 8, :].astype(f32)
         fill = fill + tile
         code = code + jnp.where(tile > 0.0, (sub8 + (2 * peer + 1)).astype(f32), 0.0)
     fill = jnp.broadcast_to(jnp.sum(fill, axis=0, keepdims=True), (8, slots))
@@ -167,9 +196,9 @@
             score_ref[t, g * 8 : (g + 1) * 8, :] = jnp.where(live, picked * SCALE, LOWEST_SCORE)
         return carry
 
-    for c in range(CHUNKS):
-        loads[0][c].wait()
-        lax.fori_loop(c * step, (c + 1) * step, score_step, 0, unroll=True)
+    for first, size, copy in key_loads:
+        copy.wait()
+        lax.fori_loop(first, first + size, score_step, 0, unroll=UNROLL)
 
     owner_h = jnp.broadcast_to(owner[0:1], (heads, slots))
     fill_h = jnp.broadcast_to(fill[0:1], (heads, slots))
@@ -204,8 +233,8 @@
         jnp.sum(jnp.where(owner_h == float(r + 1), page_sum, 0.0), axis=1, keepdims=True)
         for r in range(requests)
     ]
-    for c in range(CHUNKS):
-        loads[1][c].wait()
+    for _, _, copy in value_loads:
+        copy.wait()
     scales = []
     for g in range(groups):
         acc = jnp.zeros((requests * 8, HEAD_SIZE), f32)
@@ -232,7 +261,7 @@
                 r = 2 * peer + row
                 at = slice(g * 8, (g + 1) * 8)
                 columns.append((maxima[r][at], totals[r][at], scales[g][r * 8 : (r + 1) * 8]))
-        out_ref[peer, rows : rows + 16, :] = stat_tile(columns, LENDER_UNIT)
+        out_ref[peer, rows : rows + 8, :] = stat_tile(columns, LENDER_UNIT)
 
 
 LENDER_UNIT = 8.0
@@ -254,15 +283,14 @@
     part = jnp.round((total - whole) * PART)
     tile = jnp.where(lane < tiles, top, jnp.where(lane < 2 * tiles, whole, part))
     tile = jnp.where(lane < 3 * tiles, tile, scale)
-    tile = tile.astype(jnp.int32)
-    return jnp.concatenate([tile, jnp.zeros_like(tile)], axis=0).astype(jnp.int16)
+    return tile.astype(jnp.int32).astype(jnp.int16)
 
 
 def merge(parts_ref, groups, unit):
     tiles = 2 * groups
     count = parts_ref.shape[0]
     stats = [
-        parts_ref[i, tiles * 8 : tiles * 8 + 16, :].astype(jnp.int32).astype(f32)[0:8]
+        parts_ref[i, tiles * 8 : tiles * 8 + 8, :].astype(jnp.int32).astype(f32)
         for i in range(count)
     ]
     top = stats[0]
@@ -300,32 +328,7 @@
     for i in range(out_ref.shape[0]):
         for g in range(groups):
             out_ref[i, g * 16 : (g + 1) * 16, :] = coded[g][1]
-        out_ref[i, tiles * 8 : tiles * 8 + 16, :] = stat
-
-
-def new_token_kernel(groups, queries_ref, fresh_ref, out_ref):
-    sub = lax.broadcasted_iota(jnp.int32, (8, HEAD_SIZE), 0)
-    lane = lax.broadcasted_iota(jnp.int32, (8, HEAD_SIZE), 1)
-    fresh_k = fresh_ref[0].astype(f32)
-    fresh_v = fresh_ref[1].astype(f32)
-    values = jnp.zeros((8, HEAD_SIZE), f32)
-    tile = jnp.zeros((8, HEAD_SIZE), f32)
-    for g in range(groups):
-        both = [
-            queries_ref[:, (g * 8 + h) * HEAD_SIZE : (g * 8 + h + 1) * HEAD_SIZE].astype(f32)
-            for h in range(8)
-        ]
-        for row in range(2):
-            q = jnp.zeros((8, HEAD_SIZE), f32)
-            for h in range(8):
-                q = jnp.where(sub == h, both[h][row : row + 1, :], q)
-            k = fresh_k[row : row + 1, g * HEAD_SIZE : (g + 1) * HEAD_SIZE]
-            new = jnp.sum(q * k, axis=1, keepdims=True) * SCALE
-            tile = jnp.where(lane == g * 2 + row, new, tile)
-            v = fresh_v[row : row + 1, g * HEAD_SIZE : (g + 1) * HEAD_SIZE]
-            values = jnp.where(sub == g * 2 + row, v, values)
-    out_ref[0:8, :] = tile
-    out_ref[8:16, :] = values
+        out_ref[i, tiles * 8 : tiles * 8 + 8, :] = stat
 
 
 def finish_kernel(groups, parts_ref, token_ref, out_ref):
@@ -362,18 +365,21 @@
 
     to_send = pl.pallas_call(
         functools.partial(send_kernel, slots, pages),
-        out_shape=jax.ShapeDtypeStruct((lenders, rows + 16, HEAD_SIZE), bf16),
+        out_shape=jax.ShapeDtypeStruct((lenders, rows + 8, HEAD_SIZE), bf16),
         in_specs=[pl.BlockSpec(memory_space=SMEM)] * 2 + vmem_specs(2),
         out_specs=pl.BlockSpec(memory_space=VMEM),
         name="send",
     )(page_index, lengths, queries, block_table)
     received = lax.all_to_all(to_send, "inst", 0, 0)
 
-    kv = pl.pallas_call(
+    kv, token = pl.pallas_call(
         token_major_kernel,
-        out_shape=jax.ShapeDtypeStruct((2, page_tok, slots, width), bf16),
-        in_specs=[pl.BlockSpec(memory_space=pl.ANY)],
-        out_specs=pl.BlockSpec(memory_space=pl.ANY),
+        out_shape=(
+            jax.ShapeDtypeStruct((2, page_tok, slots, width), bf16),
+            jax.ShapeDtypeStruct((16, HEAD_SIZE), f32),
+        ),
+        in_specs=[pl.BlockSpec(memory_space=pl.ANY)] + vmem_specs(2),
+        out_specs=(pl.BlockSpec(memory_space=pl.ANY), pl.BlockSpec(memory_space=VMEM)),
         scratch_shapes=[
             pltpu.VMEM(key_value_pool.shape, bf16),
             pltpu.VMEM((2, page_tok, slots, width), bf16),
@@ -382,18 +388,18 @@
         ],
         cost_estimate=pl.CostEstimate(flops=10**9, bytes_accessed=2 * 4 * 2**20, transcendentals=0),
         name="token_major",
-    )(key_value_pool)
+    )(key_value_pool, queries, fresh_key_value)
 
     partial = pl.pallas_call(
         attend_kernel,
-        out_shape=jax.ShapeDtypeStruct((lenders, rows + 16, HEAD_SIZE), jnp.int16),
+        out_shape=jax.ShapeDtypeStruct((lenders, rows + 8, HEAD_SIZE), jnp.int16),
         in_specs=vmem_specs(1) + [pl.BlockSpec(memory_space=pltpu.MemorySpace.HBM)],
         out_specs=pl.BlockSpec(memory_space=VMEM),
         scratch_shapes=[
             pltpu.VMEM(kv.shape, bf16),
             pltpu.VMEM((page_tok, groups * 8, slots), f32),
             pltpu.VMEM((page_tok, groups * 8, slots), f32),
-            pltpu.SemaphoreType.DMA((2, CHUNKS)),
+            pltpu.SemaphoreType.DMA((len(KEY_LOADS) + len(VALUE_LOADS),)),
         ],
         compiler_params=pltpu.CompilerParams(vmem_limit_bytes=52 * 2**20),
         name="attend",
@@ -402,24 +408,13 @@
 
     combined = pl.pallas_call(
         functools.partial(combine_kernel, groups),
-        out_shape=jax.ShapeDtypeStruct((pages, rows + 16, HEAD_SIZE), jnp.int16),
+        out_shape=jax.ShapeDtypeStruct((pages, rows + 8, HEAD_SIZE), jnp.int16),
         in_specs=vmem_specs(1),
         out_specs=pl.BlockSpec(memory_space=VMEM),
         compiler_params=pltpu.CompilerParams(vmem_limit_bytes=16 * 2**20),
         name="combine",
     )(parts)
-    combined, last_queries, last_fresh = lax.optimization_barrier(
-        (combined, queries, fresh_key_value)
-    )
     page_parts = lax.all_to_all(combined, "page", 0, 0)
-    token = pl.pallas_call(
-        functools.partial(new_token_kernel, groups),
-        out_shape=jax.ShapeDtypeStruct((16, HEAD_SIZE), f32),
-        in_specs=vmem_specs(2),
-        out_specs=pl.BlockSpec(memory_space=VMEM),
-        cost_estimate=pl.CostEstimate(flops=10**6, bytes_accessed=2**16, transcendentals=0),
-        name="new_token",
-    )(last_queries, last_fresh)
 
     return pl.pallas_call(
         functools.partial(finish_kernel, groups),

time: 55.8 us -> 53.3 us (0.955)
  blocking collectives: 12.3 us -> 29.7 us
  waiting for transfers between devices: 11.6 us -> 1.94 us
  starting transfers between devices: 15.9 us -> 7.39 us
  Pallas kernels: 14.9 us -> 13.9 us
  local copies, waits for them, and re-layouts: 0.7 us -> 0.01 us
    all_to_all x0 -> x1, blocking collectives: none -> 17.5 us  [shards(): page_parts = lax.all_to_all(combined, 'page', 0, 0)]
    all_to_all x1 -> x0, starting transfers between devices: 8.46 us -> none  [shards(): page_parts = lax.all_to_all(combined, 'page', 0, 0)]
    all_to_all x1 -> x0, waiting for transfers between devices: 8.01 us -> none  [shards(): page_parts = lax.all_to_all(combined, 'page', 0, 0)]
    all_to_all x1, waiting for transfers between devices: 3.63 us -> 1.94 us  [shards(): received = lax.all_to_all(to_send, 'inst', 0, 0)]
    unnamed x2, local copies, waits for them, and re-layouts: 0.7 us -> 0.01 us
    pallas_call x1, Pallas kernels: 1.13 us -> 0.47 us  [shards(): pl.pallas_call(functools.partial(combine_kernel, groups), out_shape=jax.S...]
    pallas_call x2 -> x1, Pallas kernels: 5.44 us -> 5.4 us  [shards(): pl.pallas_call(token_major_kernel, out_shape=(jax.ShapeDtypeStruct((2, pa...]
  transfers between devices with their start and end apart: 2 -> 1, of which waited for: 2 -> 1; matrix products, arithmetic and copies ran while one was open for 0% -> 0% of each run, Pallas kernels for 10% -> 10%
where the time goes in v6:
time: 53.3 us; the launch traced here: 53 us
  blocking collectives  29.7 us (56%)
  Pallas kernels  13.9 us (26%)
  starting transfers between devices  7.39 us (14%)
  waiting for transfers between devices  1.94 us (4%)
    all_to_all x1, blocking collectives, shards(): page_parts = lax.all_to_all(combined, 'page', 0, 0)  17.5 us
    all_to_all x1, blocking collectives, shards(): parts = lax.all_to_all(partial, 'inst', 0, 0)  12.2 us
    all_to_all x1, starting transfers between devices, shards(): received = lax.all_to_all(to_send, 'inst', 0, 0)  7.39 us
    pallas_call x1, Pallas kernels, shards(): pl.pallas_call(attend_kernel, out_shape=jax.ShapeDtypeStruct((lenders, ro...  5.41 us
    pallas_call x1, Pallas kernels, shards(): pl.pallas_call(token_major_kernel, out_shape=(jax.ShapeDtypeStruct((2, pa...  5.4 us
    all_to_all x1, waiting for transfers between devices, shards(): received = lax.all_to_all(to_send, 'inst', 0, 0)  1.94 us
    pallas_call x1, Pallas kernels, shards(): pl.pallas_call(functools.partial(send_kernel, slots, pages), out_shape=ja...  1.72 us
  transfers between devices with their start and end apart: 1, of which 1 were waited for; matrix products, arithmetic and copies ran while one was open for 0% of the time, Pallas kernels for 10%

profile of v6, /device:TPU:8, one launch (start us, length us, event | category | flops | bytes accessed | tf_op | source)
XLA Modules:
  0.0 53.0 jit_solution(5865957020311140535)
XLA Ops:
  0.0 1.7 %send.1 = bf16[16,72,128]{2,1,0:T(8,128)(2,1)} custom-call(s32[1]{0:T(128)} %bitcast.page_ref, s32[2]{0:T(128)} %lengths_ref.1, bf16[2,4096]{1,0:T(2,128)(2,1)} %queries_ref.3, s32[2,768]{1,0:T(2,128)} %table_ref.1), custom_call_target="tpu_custom_call" | custom-call | tf_op jit(solution)/shard_map/send/pallas_call | solution.py:366
  1.7 7.4 %all-to-all-start = ((bf16[16,72,128]{2,1,0:T(8,128)(2,1)}), bf16[16,72,128]{2,1,0:T(8,128)(2,1)S(1)}, u32[]{:S(2)}, u32[]{:S(2)}) async-start(bf16[16,72,128]{2,1,0:T(8,128)(2,1)} %send.1), calls=%async_computation | async-start | bytes 589824 | tf_op jit(solution)/shard_map/all_to_all | solution.py:373
  9.1 5.4 %token_major.1 = (bf16[2,16,128,512]{3,2,1,0:T(8,128)(2,1)}, f32[16,128]{1,0:T(8,128)}) custom-call(bf16[2,128,16,512]{3,2,1,0:T(8,128)(2,1)} %pool_hbm.1, bf16[2,4096]{1,0:T(2,128)(2,1)} %queries_ref.3, bf16[2,2,512]{2,1,0:T(2,128)(2,1)} %fresh_ref.1), custom_call_target="tpu_custom_call" | custom-call | flops 1000000000 | bytes 8388608 | tf_op jit(solution)/shard_map/token_major/pallas_call | solution.py:375
  14.5 0.0 copy-start
  14.5 1.9 %all-to-all-done.recv_ref = bf16[16,72,128]{2,1,0:T(8,128)(2,1)S(1)} async-done(((bf16[16,72,128]{2,1,0:T(8,128)(2,1)}), bf16[16,72,128]{2,1,0:T(8,128)(2,1)S(1)}, u32[]{:S(2)}, u32[]{:S(2)}) %all-to-all-start) | async-done | bytes 294944 | tf_op jit(solution)/shard_map/all_to_all | solution.py:373
  16.5 5.4 %attend.1 = s16[16,72,128]{2,1,0:T(8,128)(2,1)S(1)} custom-call(bf16[16,72,128]{2,1,0:T(8,128)(2,1)S(1)} %all-to-all-done.recv_ref, bf16[2,16,128,512]{3,2,1,0:T(8,128)(2,1)} %get-tuple-element.7.kv_hbm), custom_call_target="tpu_custom_call" | custom-call | tf_op jit(solution)/shard_map/attend/pallas_call | solution.py:393
  21.9 12.2 %all_to_all.15.parts_ref = s16[16,72,128]{2,1,0:T(8,128)(2,1)S(1)} all-to-all(s16[16,72,128]{2,1,0:T(8,128)(2,1)S(1)} %attend.1), channel_id=1, replica_groups=mesh['inst'=16,'page'=8,'head'=2] {'inst'}, dimensions={0} | all-to-all | bytes 589824 | tf_op jit(solution)/shard_map/all_to_all | solution.py:407
  34.1 0.5 combine.1
  34.6 17.5 %all_to_all.16.parts_ref = s16[8,72,128]{2,1,0:T(8,128)(2,1)S(1)} all-to-all(s16[8,72,128]{2,1,0:T(8,128)(2,1)S(1)} %combine.1), channel_id=1, replica_groups=mesh['inst'=16,'page'=8,'head'=2] {'page'}, dimensions={0} | all-to-all | bytes 294912 | tf_op jit(solution)/shard_map/all_to_all | solution.py:417
  52.1 0.0 copy-done
  52.1 0.9 %finish.1 = bf16[2,4096]{1,0:T(2,128)(2,1)} custom-call(s16[8,72,128]{2,1,0:T(8,128)(2,1)S(1)} %all_to_all.16.parts_ref, f32[16,128]{1,0:T(8,128)S(1)} %copy-done), custom_call_target="tpu_custom_call" | custom-call | tf_op jit(solution)/shard_map/finish/pallas_call | solution.py:419
Async XLA Ops:
  1.7 14.8 %all-to-all-start = ((bf16[16,72,128]{2,1,0:T(8,128)(2,1)}), bf16[16,72,128]{2,1,0:T(8,128)(2,1)S(1)}, u32[]{:S(2)}, u32[]{:S(2)}) async-start(bf16[16,72,128]{2,1,0:T(8,128)(2,1)} %send.1), calls=%async_computation | async-start | bytes 589824 | tf_op jit(solution)/shard_map/all_to_all | solution.py:373
  14.5 37.6 %copy-start = (f32[16,128]{1,0:T(8,128)S(1)}, f32[16,128]{1,0:T(8,128)}, u32[]{:S(2)}) copy-start(f32[16,128]{1,0:T(8,128)} %get-tuple-element.8.token_ref) | copy-start | bytes 24580

commit v7 on v6

--- a/solution.py
+++ b/solution.py
@@ -110,7 +110,19 @@
 
 
 def token_major_kernel(
-    pool_hbm, queries_ref, fresh_ref, out_hbm, token_ref, pool_ref, out_ref, load_sems, store_sems
+    pool_hbm,
+    queries_hbm,
+    fresh_hbm,
+    out_hbm,
+    token_hbm,
+    pool_ref,
+    queries_ref,
+    fresh_ref,
+    out_ref,
+    token_ref,
+    load_sems,
+    store_sems,
+    token_sems,
 ):
     pages, page_tok, width = pool_hbm.shape[1:]
     chunk = pages // PARTS
@@ -132,13 +144,24 @@
             )
     for load in loads:
         load.start()
+    small = [
+        pltpu.make_async_copy(queries_hbm, queries_ref, token_sems.at[0]),
+        pltpu.make_async_copy(fresh_hbm, fresh_ref, token_sems.at[1]),
+    ]
+    for load in small:
+        load.start()
     i = lax.broadcasted_iota(jnp.int32, (block, block), 0)
     j = lax.broadcasted_iota(jnp.int32, (block, block), 1)
-    new_token(queries_ref, fresh_ref, token_ref)
     perm = jnp.where((i % 16) * page_tok + i // 16 == j, 1.0, 0.0).astype(bf16)
     for kind in range(2):
         for c in range(PARTS):
             loads[kind * PARTS + c].wait()
+            if kind == 1 and c == PARTS - 1:
+                for load in small:
+                    load.wait()
+                new_token(queries_ref, fresh_ref, token_ref)
+                stores.append(pltpu.make_async_copy(token_ref, token_hbm, token_sems.at[2]))
+                stores[-1].start()
             for b in range(chunk // 16):
                 first = c * chunk + b * 16
                 rows = pool_ref[kind, first : first + 16].reshape(block, width)
@@ -200,6 +223,8 @@
         copy.wait()
         lax.fori_loop(first, first + size, score_step, 0, unroll=UNROLL)
 
+    for _, _, copy in value_loads:
+        copy.wait()
     owner_h = jnp.broadcast_to(owner[0:1], (heads, slots))
     fill_h = jnp.broadcast_to(fill[0:1], (heads, slots))
     page_max = score_ref[0]
@@ -233,8 +258,6 @@
         jnp.sum(jnp.where(owner_h == float(r + 1), page_sum, 0.0), axis=1, keepdims=True)
         for r in range(requests)
     ]
-    for _, _, copy in value_loads:
-        copy.wait()
     scales = []
     for g in range(groups):
         acc = jnp.zeros((requests * 8, HEAD_SIZE), f32)
@@ -378,13 +401,17 @@
             jax.ShapeDtypeStruct((2, page_tok, slots, width), bf16),
             jax.ShapeDtypeStruct((16, HEAD_SIZE), f32),
         ),
-        in_specs=[pl.BlockSpec(memory_space=pl.ANY)] + vmem_specs(2),
-        out_specs=(pl.BlockSpec(memory_space=pl.ANY), pl.BlockSpec(memory_space=VMEM)),
+        in_specs=[pl.BlockSpec(memory_space=pl.ANY)] * 3,
+        out_specs=(pl.BlockSpec(memory_space=pl.ANY),) * 2,
         scratch_shapes=[
             pltpu.VMEM(key_value_pool.shape, bf16),
+            pltpu.VMEM(queries.shape, bf16),
+            pltpu.VMEM(fresh_key_value.shape, bf16),
             pltpu.VMEM((2, page_tok, slots, width), bf16),
+            pltpu.VMEM((16, HEAD_SIZE), f32),
             pltpu.SemaphoreType.DMA((2, PARTS)),
             pltpu.SemaphoreType.DMA((2, PARTS)),
+            pltpu.SemaphoreType.DMA((3,)),
         ],
         cost_estimate=pl.CostEstimate(flops=10**9, bytes_accessed=2 * 4 * 2**20, transcendentals=0),
         name="token_major",

time: 53.3 us -> 52.9 us (level)
  Pallas kernels: 13.9 us -> 12.4 us
  waiting for transfers between devices: 1.94 us -> 3.23 us
    all_to_all x1, waiting for transfers between devices: 1.94 us -> 3.23 us  [shards(): received = lax.all_to_all(to_send, 'inst', 0, 0)]
    pallas_call x1, Pallas kernels: 5.4 us -> 4.11 us  [shards(): pl.pallas_call(token_major_kernel, out_shape=(jax.ShapeDtypeStruct((2, pa...]
  transfers between devices with their start and end apart: 1 -> 1, of which waited for: 1 -> 1; matrix products, arithmetic and copies ran while one was open for 0% -> 0% of each run, Pallas kernels for 10% -> 8%
where the time goes in v7:
time: 52.9 us; the launch traced here: 52.6 us
  blocking collectives  29.5 us (56%)
  Pallas kernels  12.4 us (23%)
  starting transfers between devices  7.39 us (14%)
  waiting for transfers between devices  3.23 us (6%)
    all_to_all x1, blocking collectives, shards(): page_parts = lax.all_to_all(combined, 'page', 0, 0)  17.5 us
    all_to_all x1, blocking collectives, shards(): parts = lax.all_to_all(partial, 'inst', 0, 0)  12 us
    all_to_all x1, starting transfers between devices, shards(): received = lax.all_to_all(to_send, 'inst', 0, 0)  7.39 us
    pallas_call x1, Pallas kernels, shards(): pl.pallas_call(attend_kernel, out_shape=jax.ShapeDtypeStruct((lenders, ro...  5.21 us
    pallas_call x1, Pallas kernels, shards(): pl.pallas_call(token_major_kernel, out_shape=(jax.ShapeDtypeStruct((2, pa...  4.11 us
    all_to_all x1, waiting for transfers between devices, shards(): received = lax.all_to_all(to_send, 'inst', 0, 0)  3.23 us
    pallas_call x1, Pallas kernels, shards(): pl.pallas_call(functools.partial(send_kernel, slots, pages), out_shape=ja...  1.72 us
  transfers between devices with their start and end apart: 1, of which 1 were waited for; matrix products, arithmetic and copies ran while one was open for 0% of the time, Pallas kernels for 8%

profile of v7, /device:TPU:8, one launch (start us, length us, event | category | flops | bytes accessed | tf_op | source)
XLA Modules:
  0.0 52.6 jit_solution(13664914999265404013)
XLA Ops:
  0.0 1.7 %send.1 = bf16[16,72,128]{2,1,0:T(8,128)(2,1)} custom-call(s32[1]{0:T(128)} %bitcast.page_ref, s32[2]{0:T(128)} %lengths_ref.1, bf16[2,4096]{1,0:T(2,128)(2,1)} %queries_hbm.1, s32[2,768]{1,0:T(2,128)} %table_ref.1), custom_call_target="tpu_custom_call" | custom-call | tf_op jit(solution)/shard_map/send/pallas_call | solution.py:389
  1.7 7.4 %all-to-all-start = ((bf16[16,72,128]{2,1,0:T(8,128)(2,1)}), bf16[16,72,128]{2,1,0:T(8,128)(2,1)S(1)}, u32[]{:S(2)}, u32[]{:S(2)}) async-start(bf16[16,72,128]{2,1,0:T(8,128)(2,1)} %send.1), calls=%async_computation | async-start | bytes 589824 | tf_op jit(solution)/shard_map/all_to_all | solution.py:396
  9.1 4.1 %token_major.1 = (bf16[2,16,128,512]{3,2,1,0:T(8,128)(2,1)}, f32[16,128]{1,0:T(8,128)}) custom-call(bf16[2,128,16,512]{3,2,1,0:T(8,128)(2,1)} %pool_hbm.1, bf16[2,4096]{1,0:T(2,128)(2,1)} %queries_hbm.1, bf16[2,2,512]{2,1,0:T(2,128)(2,1)} %fresh_hbm.1), custom_call_target="tpu_custom_call" | custom-call | flops 1000000000 | bytes 8388608 | tf_op jit(solution)/shard_map/token_major/pallas_call | solution.py:398
  13.2 0.0 copy-start
  13.2 3.2 %all-to-all-done.recv_ref = bf16[16,72,128]{2,1,0:T(8,128)(2,1)S(1)} async-done(((bf16[16,72,128]{2,1,0:T(8,128)(2,1)}), bf16[16,72,128]{2,1,0:T(8,128)(2,1)S(1)}, u32[]{:S(2)}, u32[]{:S(2)}) %all-to-all-start) | async-done | bytes 294944 | tf_op jit(solution)/shard_map/all_to_all | solution.py:396
  16.5 5.2 %attend.1 = s16[16,72,128]{2,1,0:T(8,128)(2,1)S(1)} custom-call(bf16[16,72,128]{2,1,0:T(8,128)(2,1)S(1)} %all-to-all-done.recv_ref, bf16[2,16,128,512]{3,2,1,0:T(8,128)(2,1)} %get-tuple-element.7.kv_hbm), custom_call_target="tpu_custom_call" | custom-call | tf_op jit(solution)/shard_map/attend/pallas_call | solution.py:420
  21.7 12.0 %all_to_all.15.parts_ref = s16[16,72,128]{2,1,0:T(8,128)(2,1)S(1)} all-to-all(s16[16,72,128]{2,1,0:T(8,128)(2,1)S(1)} %attend.1), channel_id=1, replica_groups=mesh['inst'=16,'page'=8,'head'=2] {'inst'}, dimensions={0} | all-to-all | bytes 589824 | tf_op jit(solution)/shard_map/all_to_all | solution.py:434
  33.7 0.5 combine.1
  34.2 17.5 %all_to_all.16.parts_ref = s16[8,72,128]{2,1,0:T(8,128)(2,1)S(1)} all-to-all(s16[8,72,128]{2,1,0:T(8,128)(2,1)S(1)} %combine.1), channel_id=1, replica_groups=mesh['inst'=16,'page'=8,'head'=2] {'page'}, dimensions={0} | all-to-all | bytes 294912 | tf_op jit(solution)/shard_map/all_to_all | solution.py:444
  51.7 0.0 copy-done
  51.7 0.9 %finish.1 = bf16[2,4096]{1,0:T(2,128)(2,1)} custom-call(s16[8,72,128]{2,1,0:T(8,128)(2,1)S(1)} %all_to_all.16.parts_ref, f32[16,128]{1,0:T(8,128)S(1)} %copy-done), custom_call_target="tpu_custom_call" | custom-call | tf_op jit(solution)/shard_map/finish/pallas_call | solution.py:446
Async XLA Ops:
  1.7 14.8 %all-to-all-start = ((bf16[16,72,128]{2,1,0:T(8,128)(2,1)}), bf16[16,72,128]{2,1,0:T(8,128)(2,1)S(1)}, u32[]{:S(2)}, u32[]{:S(2)}) async-start(bf16[16,72,128]{2,1,0:T(8,128)(2,1)} %send.1), calls=%async_computation | async-start | bytes 589824 | tf_op jit(solution)/shard_map/all_to_all | solution.py:396
  13.2 38.5 %copy-start = (f32[16,128]{1,0:T(8,128)S(1)}, f32[16,128]{1,0:T(8,128)}, u32[]{:S(2)}) copy-start(f32[16,128]{1,0:T(8,128)} %get-tuple-element.8.token_ref) | copy-start | bytes 24580

commit v8 on v6

--- a/solution.py
+++ b/solution.py
@@ -110,14 +110,14 @@
 
 
 def token_major_kernel(
-    pool_hbm, queries_ref, fresh_ref, out_hbm, token_ref, pool_ref, out_ref, load_sems, store_sems
+    pool_hbm, keys_ref, values_hbm, pool_ref, values_ref, load_sems, store_sems
 ):
     pages, page_tok, width = pool_hbm.shape[1:]
     chunk = pages // PARTS
     block = page_tok * 16
     loads = []
     stores = []
-    for kind in range(2):
+    for kind in (1, 0):
         for c in range(PARTS):
             at = pl.ds(c * chunk, chunk)
             loads.append(
@@ -125,51 +125,49 @@
                     pool_hbm.at[kind, at], pool_ref.at[kind, at], load_sems.at[kind, c]
                 )
             )
-            stores.append(
-                pltpu.make_async_copy(
-                    out_ref.at[kind, :, at], out_hbm.at[kind, :, at], store_sems.at[kind, c]
+            if kind == 1:
+                stores.append(
+                    pltpu.make_async_copy(
+                        values_ref.at[:, at], values_hbm.at[:, at], store_sems.at[c]
+                    )
                 )
-            )
     for load in loads:
         load.start()
     i = lax.broadcasted_iota(jnp.int32, (block, block), 0)
     j = lax.broadcasted_iota(jnp.int32, (block, block), 1)
-    new_token(queries_ref, fresh_ref, token_ref)
     perm = jnp.where((i % 16) * page_tok + i // 16 == j, 1.0, 0.0).astype(bf16)
-    for kind in range(2):
+    for kind in (1, 0):
+        out_ref = values_ref if kind == 1 else keys_ref
         for c in range(PARTS):
-            loads[kind * PARTS + c].wait()
+            loads[(1 - kind) * PARTS + c].wait()
             for b in range(chunk // 16):
                 first = c * chunk + b * 16
                 rows = pool_ref[kind, first : first + 16].reshape(block, width)
                 moved = jnp.dot(perm, rows, preferred_element_type=f32).astype(bf16)
-                out_ref[kind, :, first : first + 16, :] = moved.reshape(page_tok, 16, width)
-            stores[kind * PARTS + c].start()
+                out_ref[:, first : first + 16, :] = moved.reshape(page_tok, 16, width)
+            if kind == 1:
+                stores[c].start()
     for store in stores:
         store.wait()
 
 
-KEY_LOADS = (4, 12)
-VALUE_LOADS = (16,)
-UNROLL = True
-
-
-def attend_kernel(recv_ref, kv_hbm, out_ref, kv_ref, score_ref, weight_ref, sems):
+def attend_kernel(
+    recv_ref,
+    keys_ref,
+    queries_ref,
+    fresh_ref,
+    values_hbm,
+    out_ref,
+    token_ref,
+    values_ref,
+    score_ref,
+    weight_ref,
+    sem,
+):
     peers = recv_ref.shape[0]
-    page_tok, slots, width = kv_ref.shape[1:]
-    loads = []
-    for kind, sizes in enumerate((KEY_LOADS, VALUE_LOADS)):
-        first = 0
-        for size in sizes:
-            at = pl.ds(first, size)
-            copy = pltpu.make_async_copy(
-                kv_hbm.at[kind, at], kv_ref.at[kind, at], sems.at[len(loads)]
-            )
-            copy.start()
-            loads.append((first, size, copy))
-            first += size
-    key_loads = loads[: len(KEY_LOADS)]
-    value_loads = loads[len(KEY_LOADS) :]
+    page_tok, slots, width = keys_ref.shape
+    load = pltpu.make_async_copy(values_hbm, values_ref, sem)
+    load.start()
     groups = width // HEAD_SIZE
     requests = 2 * peers
     heads = groups * 8
@@ -188,7 +186,7 @@
         live = fill > jnp.asarray(t, f32)
         for g in range(groups):
             q = recv_ref[:, g * 16 : (g + 1) * 16, :].reshape(requests * 8, HEAD_SIZE)
-            k = kv_ref[0, t, :, g * HEAD_SIZE : (g + 1) * HEAD_SIZE]
+            k = keys_ref[t, :, g * HEAD_SIZE : (g + 1) * HEAD_SIZE]
             s = nt_dot(q, k)
             picked = jnp.zeros((8, slots), f32)
             for r in range(requests):
@@ -196,10 +194,10 @@
             score_ref[t, g * 8 : (g + 1) * 8, :] = jnp.where(live, picked * SCALE, LOWEST_SCORE)
         return carry
 
-    for first, size, copy in key_loads:
-        copy.wait()
-        lax.fori_loop(first, first + size, score_step, 0, unroll=UNROLL)
-
+    lax.fori_loop(0, page_tok, score_step, 0, unroll=True)
+
+    load.wait()
+    new_token(queries_ref, fresh_ref, token_ref)
     owner_h = jnp.broadcast_to(owner[0:1], (heads, slots))
     fill_h = jnp.broadcast_to(fill[0:1], (heads, slots))
     page_max = score_ref[0]
@@ -233,13 +231,11 @@
         jnp.sum(jnp.where(owner_h == float(r + 1), page_sum, 0.0), axis=1, keepdims=True)
         for r in range(requests)
     ]
-    for _, _, copy in value_loads:
-        copy.wait()
     scales = []
     for g in range(groups):
         acc = jnp.zeros((requests * 8, HEAD_SIZE), f32)
         for t0 in range(0, page_tok, 2):
-            v = kv_ref[1, t0 : t0 + 2, :, g * HEAD_SIZE : (g + 1) * HEAD_SIZE].reshape(
+            v = values_ref[t0 : t0 + 2, :, g * HEAD_SIZE : (g + 1) * HEAD_SIZE].reshape(
                 2 * slots, HEAD_SIZE
             )
             for ref in (score_ref, weight_ref):
@@ -372,38 +368,42 @@
     )(page_index, lengths, queries, block_table)
     received = lax.all_to_all(to_send, "inst", 0, 0)
 
-    kv, token = pl.pallas_call(
+    keys, values = pl.pallas_call(
         token_major_kernel,
         out_shape=(
-            jax.ShapeDtypeStruct((2, page_tok, slots, width), bf16),
+            jax.ShapeDtypeStruct((page_tok, slots, width), bf16),
+            jax.ShapeDtypeStruct((page_tok, slots, width), bf16),
+        ),
+        in_specs=[pl.BlockSpec(memory_space=pl.ANY)],
+        out_specs=(pl.BlockSpec(memory_space=VMEM), pl.BlockSpec(memory_space=pl.ANY)),
+        scratch_shapes=[
+            pltpu.VMEM(key_value_pool.shape, bf16),
+            pltpu.VMEM((page_tok, slots, width), bf16),
+            pltpu.SemaphoreType.DMA((2, PARTS)),
+            pltpu.SemaphoreType.DMA((PARTS,)),
+        ],
+        cost_estimate=pl.CostEstimate(flops=10**9, bytes_accessed=2 * 4 * 2**20, transcendentals=0),
+        compiler_params=pltpu.CompilerParams(vmem_limit_bytes=50 * 2**20),
+        name="token_major",
+    )(key_value_pool)
+
+    partial, token = pl.pallas_call(
+        attend_kernel,
+        out_shape=(
+            jax.ShapeDtypeStruct((lenders, rows + 8, HEAD_SIZE), jnp.int16),
             jax.ShapeDtypeStruct((16, HEAD_SIZE), f32),
         ),
-        in_specs=[pl.BlockSpec(memory_space=pl.ANY)] + vmem_specs(2),
-        out_specs=(pl.BlockSpec(memory_space=pl.ANY), pl.BlockSpec(memory_space=VMEM)),
+        in_specs=vmem_specs(4) + [pl.BlockSpec(memory_space=pl.ANY)],
+        out_specs=tuple(vmem_specs(2)),
         scratch_shapes=[
-            pltpu.VMEM(key_value_pool.shape, bf16),
-            pltpu.VMEM((2, page_tok, slots, width), bf16),
-            pltpu.SemaphoreType.DMA((2, PARTS)),
-            pltpu.SemaphoreType.DMA((2, PARTS)),
-        ],
-        cost_estimate=pl.CostEstimate(flops=10**9, bytes_accessed=2 * 4 * 2**20, transcendentals=0),
-        name="token_major",
-    )(key_value_pool, queries, fresh_key_value)
-
-    partial = pl.pallas_call(
-        attend_kernel,
-        out_shape=jax.ShapeDtypeStruct((lenders, rows + 8, HEAD_SIZE), jnp.int16),
-        in_specs=vmem_specs(1) + [pl.BlockSpec(memory_space=pltpu.MemorySpace.HBM)],
-        out_specs=pl.BlockSpec(memory_space=VMEM),
-        scratch_shapes=[
-            pltpu.VMEM(kv.shape, bf16),
+            pltpu.VMEM(values.shape, bf16),
             pltpu.VMEM((page_tok, groups * 8, slots), f32),
             pltpu.VMEM((page_tok, groups * 8, slots), f32),
-            pltpu.SemaphoreType.DMA((len(KEY_LOADS) + len(VALUE_LOADS),)),
+            pltpu.SemaphoreType.DMA,
         ],
-        compiler_params=pltpu.CompilerParams(vmem_limit_bytes=52 * 2**20),
+        compiler_params=pltpu.CompilerParams(vmem_limit_bytes=51 * 2**20),
         name="attend",
-    )(received, kv)
+    )(received, keys, queries, fresh_key_value, values)
     parts = lax.all_to_all(partial, "inst", 0, 0)
 
     combined = pl.pallas_call(

time: 53.3 us -> 53.1 us (level)
  Pallas kernels: 13.9 us -> 11.6 us
  waiting for transfers between devices: 1.94 us -> 4.19 us
    pallas_call x2, Pallas kernels: 10.8 us -> 8.56 us  [the longest x1 5.4 us: shards(): pl.pallas_call(attend_kernel, out_shape=(jax.ShapeDtypeStruct((lenders, r...]
    all_to_all x1, waiting for transfers between devices: 1.94 us -> 4.19 us  [shards(): received = lax.all_to_all(to_send, 'inst', 0, 0)]
  transfers between devices with their start and end apart: 1 -> 1, of which waited for: 1 -> 1; matrix products, arithmetic and copies ran while one was open for 0% -> 0% of each run, Pallas kernels for 10% -> 6%
where the time goes in v8:
time: 53.1 us; the launch traced here: 52.8 us
  blocking collectives  29.5 us (56%)
  Pallas kernels  11.6 us (22%)
  starting transfers between devices  7.39 us (14%)
  waiting for transfers between devices  4.19 us (8%)
    all_to_all x1, blocking collectives, shards(): page_parts = lax.all_to_all(combined, 'page', 0, 0)  17.5 us
    all_to_all x1, blocking collectives, shards(): parts = lax.all_to_all(partial, 'inst', 0, 0)  12 us
    all_to_all x1, starting transfers between devices, shards(): received = lax.all_to_all(to_send, 'inst', 0, 0)  7.39 us
    pallas_call x1, Pallas kernels, shards(): pl.pallas_call(attend_kernel, out_shape=(jax.ShapeDtypeStruct((lenders, r...  5.4 us
    all_to_all x1, waiting for transfers between devices, shards(): received = lax.all_to_all(to_send, 'inst', 0, 0)  4.19 us
    pallas_call x1, Pallas kernels, shards(): pl.pallas_call(token_major_kernel, out_shape=(jax.ShapeDtypeStruct((page_...  3.16 us
    pallas_call x1, Pallas kernels, shards(): pl.pallas_call(functools.partial(send_kernel, slots, pages), out_shape=ja...  1.72 us
  transfers between devices with their start and end apart: 1, of which 1 were waited for; matrix products, arithmetic and copies ran while one was open for 0% of the time, Pallas kernels for 6%

profile of v8, /device:TPU:8, one launch (start us, length us, event | category | flops | bytes accessed | tf_op | source)
XLA Modules:
  0.0 52.8 jit_solution(10970658483085187076)
XLA Ops:
  0.0 1.7 %send.1 = bf16[16,72,128]{2,1,0:T(8,128)(2,1)} custom-call(s32[1]{0:T(128)} %bitcast.page_ref, s32[2]{0:T(128)} %lengths_ref.1, bf16[2,4096]{1,0:T(2,128)(2,1)} %queries_ref.3, s32[2,768]{1,0:T(2,128)} %table_ref.1), custom_call_target="tpu_custom_call" | custom-call | tf_op jit(solution)/shard_map/send/pallas_call | solution.py:362
  1.7 7.4 %all-to-all-start = ((bf16[16,72,128]{2,1,0:T(8,128)(2,1)}), bf16[16,72,128]{2,1,0:T(8,128)(2,1)S(1)}, u32[]{:S(2)}, u32[]{:S(2)}) async-start(bf16[16,72,128]{2,1,0:T(8,128)(2,1)} %send.1), calls=%async_computation | async-start | bytes 589824 | tf_op jit(solution)/shard_map/all_to_all | solution.py:369
  9.1 0.0 copy-start
  9.1 0.0 copy-start.1
  9.1 3.2 %token_major.1 = (bf16[16,128,512]{2,1,0:T(8,128)(2,1)S(1)}, bf16[16,128,512]{2,1,0:T(8,128)(2,1)}) custom-call(bf16[2,128,16,512]{3,2,1,0:T(8,128)(2,1)} %pool_hbm.1), custom_call_target="tpu_custom_call" | custom-call | flops 1000000000 | bytes 8388608 | tf_op jit(solution)/shard_map/token_major/pallas_call | solution.py:371
  12.3 4.2 %all-to-all-done.recv_ref = bf16[16,72,128]{2,1,0:T(8,128)(2,1)S(1)} async-done(((bf16[16,72,128]{2,1,0:T(8,128)(2,1)}), bf16[16,72,128]{2,1,0:T(8,128)(2,1)S(1)}, u32[]{:S(2)}, u32[]{:S(2)}) %all-to-all-start) | async-done | bytes 294944 | tf_op jit(solution)/shard_map/all_to_all | solution.py:369
  16.5 0.0 copy-done
  16.5 0.0 copy-done.1
  16.5 5.4 %attend.1 = (s16[16,72,128]{2,1,0:T(8,128)(2,1)S(1)}, f32[16,128]{1,0:T(8,128)S(1)}) custom-call(bf16[16,72,128]{2,1,0:T(8,128)(2,1)S(1)} %all-to-all-done.recv_ref, bf16[16,128,512]{2,1,0:T(8,128)(2,1)S(1)} %get-tuple-element.9.keys_ref, bf16[2,4096]{1,0:T(2,128)(2,1)S(1)} %copy-done, bf16[2,2,512]{2,1,0:T(2,128)(2,1)S(1)} %copy-done.1, ...), custom_call_target="tpu_custom_call" | custom-call | tf_op jit(solution)/shard_map/attend/pallas_call | solution.py:390
  21.9 12.0 %all_to_all.15.parts_ref = s16[16,72,128]{2,1,0:T(8,128)(2,1)S(1)} all-to-all(s16[16,72,128]{2,1,0:T(8,128)(2,1)S(1)} %get-tuple-element.11), channel_id=1, replica_groups=mesh['inst'=16,'page'=8,'head'=2] {'inst'}, dimensions={0} | all-to-all | bytes 589824 | tf_op jit(solution)/shard_map/all_to_all | solution.py:407
  33.9 0.5 combine.1
  34.4 17.5 %all_to_all.16.parts_ref = s16[8,72,128]{2,1,0:T(8,128)(2,1)S(1)} all-to-all(s16[8,72,128]{2,1,0:T(8,128)(2,1)S(1)} %combine.1), channel_id=1, replica_groups=mesh['inst'=16,'page'=8,'head'=2] {'page'}, dimensions={0} | all-to-all | bytes 294912 | tf_op jit(solution)/shard_map/all_to_all | solution.py:417
  51.9 0.9 %finish.1 = bf16[2,4096]{1,0:T(2,128)(2,1)} custom-call(s16[8,72,128]{2,1,0:T(8,128)(2,1)S(1)} %all_to_all.16.parts_ref, f32[16,128]{1,0:T(8,128)S(1)} %get-tuple-element.12.token_ref), custom_call_target="tpu_custom_call" | custom-call | tf_op jit(solution)/shard_map/finish/pallas_call | solution.py:419
Async XLA Ops:
  1.7 14.8 %all-to-all-start = ((bf16[16,72,128]{2,1,0:T(8,128)(2,1)}), bf16[16,72,128]{2,1,0:T(8,128)(2,1)S(1)}, u32[]{:S(2)}, u32[]{:S(2)}) async-start(bf16[16,72,128]{2,1,0:T(8,128)(2,1)} %send.1), calls=%async_computation | async-start | bytes 589824 | tf_op jit(solution)/shard_map/all_to_all | solution.py:369
  9.1 7.4 %copy-start = (bf16[2,4096]{1,0:T(2,128)(2,1)S(1)}, bf16[2,4096]{1,0:T(2,128)(2,1)}, u32[]{:S(2)}) copy-start(bf16[2,4096]{1,0:T(2,128)(2,1)} %queries_ref.3) | copy-start | bytes 49156
  9.1 7.4 %copy-start.1 = (bf16[2,2,512]{2,1,0:T(2,128)(2,1)S(1)}, bf16[2,2,512]{2,1,0:T(2,128)(2,1)}, u32[]{:S(2)}) copy-start(bf16[2,2,512]{2,1,0:T(2,128)(2,1)} %fresh_ref.1) | copy-start | bytes 12292

commit v9 on v8

--- a/solution.py
+++ b/solution.py
@@ -194,7 +194,7 @@
             score_ref[t, g * 8 : (g + 1) * 8, :] = jnp.where(live, picked * SCALE, LOWEST_SCORE)
         return carry
 
-    lax.fori_loop(0, page_tok, score_step, 0, unroll=True)
+    lax.fori_loop(0, page_tok, score_step, 0, unroll=8)
 
     load.wait()
     new_token(queries_ref, fresh_ref, token_ref)

time: 53.1 us -> 52 us (0.979)
  Pallas kernels: 11.6 us -> 10.5 us
    pallas_call x1, Pallas kernels: 5.4 us -> 4.27 us  [shards(): pl.pallas_call(attend_kernel, out_shape=(jax.ShapeDtypeStruct((lenders, r...]
where the time goes in v9:
time: 52 us; the launch traced here: 51.7 us
  blocking collectives  29.5 us (57%)
  Pallas kernels  10.5 us (20%)
  starting transfers between devices  7.39 us (14%)
  waiting for transfers between devices  4.19 us (8%)
    all_to_all x1, blocking collectives, shards(): page_parts = lax.all_to_all(combined, 'page', 0, 0)  17.5 us
    all_to_all x1, blocking collectives, shards(): parts = lax.all_to_all(partial, 'inst', 0, 0)  12 us
    all_to_all x1, starting transfers between devices, shards(): received = lax.all_to_all(to_send, 'inst', 0, 0)  7.39 us
    pallas_call x1, Pallas kernels, shards(): pl.pallas_call(attend_kernel, out_shape=(jax.ShapeDtypeStruct((lenders, r...  4.27 us
    all_to_all x1, waiting for transfers between devices, shards(): received = lax.all_to_all(to_send, 'inst', 0, 0)  4.19 us
    pallas_call x1, Pallas kernels, shards(): pl.pallas_call(token_major_kernel, out_shape=(jax.ShapeDtypeStruct((page_...  3.16 us
    pallas_call x1, Pallas kernels, shards(): pl.pallas_call(functools.partial(send_kernel, slots, pages), out_shape=ja...  1.72 us
  transfers between devices with their start and end apart: 1, of which 1 were waited for; matrix products, arithmetic and copies ran while one was open for 0% of the time, Pallas kernels for 6%

profile of v9, /device:TPU:8, one launch (start us, length us, event | category | flops | bytes accessed | tf_op | source)
XLA Modules:
  0.0 51.7 jit_solution(4764503860914539341)
XLA Ops:
  0.0 1.7 %send.1 = bf16[16,72,128]{2,1,0:T(8,128)(2,1)} custom-call(s32[1]{0:T(128)} %bitcast.page_ref, s32[2]{0:T(128)} %lengths_ref.1, bf16[2,4096]{1,0:T(2,128)(2,1)} %queries_ref.3, s32[2,768]{1,0:T(2,128)} %table_ref.1), custom_call_target="tpu_custom_call" | custom-call | tf_op jit(solution)/shard_map/send/pallas_call | solution.py:362
  1.7 7.4 %all-to-all-start = ((bf16[16,72,128]{2,1,0:T(8,128)(2,1)}), bf16[16,72,128]{2,1,0:T(8,128)(2,1)S(1)}, u32[]{:S(2)}, u32[]{:S(2)}) async-start(bf16[16,72,128]{2,1,0:T(8,128)(2,1)} %send.1), calls=%async_computation | async-start | bytes 589824 | tf_op jit(solution)/shard_map/all_to_all | solution.py:369
  9.1 0.0 copy-start
  9.1 0.0 copy-start.1
  9.1 3.2 %token_major.1 = (bf16[16,128,512]{2,1,0:T(8,128)(2,1)S(1)}, bf16[16,128,512]{2,1,0:T(8,128)(2,1)}) custom-call(bf16[2,128,16,512]{3,2,1,0:T(8,128)(2,1)} %pool_hbm.1), custom_call_target="tpu_custom_call" | custom-call | flops 1000000000 | bytes 8388608 | tf_op jit(solution)/shard_map/token_major/pallas_call | solution.py:371
  12.3 4.2 %all-to-all-done.recv_ref = bf16[16,72,128]{2,1,0:T(8,128)(2,1)S(1)} async-done(((bf16[16,72,128]{2,1,0:T(8,128)(2,1)}), bf16[16,72,128]{2,1,0:T(8,128)(2,1)S(1)}, u32[]{:S(2)}, u32[]{:S(2)}) %all-to-all-start) | async-done | bytes 294944 | tf_op jit(solution)/shard_map/all_to_all | solution.py:369
  16.5 0.0 copy-done
  16.5 0.0 copy-done.1
  16.5 4.3 %attend.1 = (s16[16,72,128]{2,1,0:T(8,128)(2,1)S(1)}, f32[16,128]{1,0:T(8,128)S(1)}) custom-call(bf16[16,72,128]{2,1,0:T(8,128)(2,1)S(1)} %all-to-all-done.recv_ref, bf16[16,128,512]{2,1,0:T(8,128)(2,1)S(1)} %get-tuple-element.9.keys_ref, bf16[2,4096]{1,0:T(2,128)(2,1)S(1)} %copy-done, bf16[2,2,512]{2,1,0:T(2,128)(2,1)S(1)} %copy-done.1, ...), custom_call_target="tpu_custom_call" | custom-call | tf_op jit(solution)/shard_map/attend/pallas_call | solution.py:390
  20.8 12.0 %all_to_all.15.parts_ref = s16[16,72,128]{2,1,0:T(8,128)(2,1)S(1)} all-to-all(s16[16,72,128]{2,1,0:T(8,128)(2,1)S(1)} %get-tuple-element.11), channel_id=1, replica_groups=mesh['inst'=16,'page'=8,'head'=2] {'inst'}, dimensions={0} | all-to-all | bytes 589824 | tf_op jit(solution)/shard_map/all_to_all | solution.py:407
  32.8 0.5 combine.1
  33.3 17.5 %all_to_all.16.parts_ref = s16[8,72,128]{2,1,0:T(8,128)(2,1)S(1)} all-to-all(s16[8,72,128]{2,1,0:T(8,128)(2,1)S(1)} %combine.1), channel_id=1, replica_groups=mesh['inst'=16,'page'=8,'head'=2] {'page'}, dimensions={0} | all-to-all | bytes 294912 | tf_op jit(solution)/shard_map/all_to_all | solution.py:417
  50.8 0.9 %finish.1 = bf16[2,4096]{1,0:T(2,128)(2,1)} custom-call(s16[8,72,128]{2,1,0:T(8,128)(2,1)S(1)} %all_to_all.16.parts_ref, f32[16,128]{1,0:T(8,128)S(1)} %get-tuple-element.12.token_ref), custom_call_target="tpu_custom_call" | custom-call | tf_op jit(solution)/shard_map/finish/pallas_call | solution.py:419
Async XLA Ops:
  1.7 14.8 %all-to-all-start = ((bf16[16,72,128]{2,1,0:T(8,128)(2,1)}), bf16[16,72,128]{2,1,0:T(8,128)(2,1)S(1)}, u32[]{:S(2)}, u32[]{:S(2)}) async-start(bf16[16,72,128]{2,1,0:T(8,128)(2,1)} %send.1), calls=%async_computation | async-start | bytes 589824 | tf_op jit(solution)/shard_map/all_to_all | solution.py:369
  9.1 7.4 %copy-start = (bf16[2,4096]{1,0:T(2,128)(2,1)S(1)}, bf16[2,4096]{1,0:T(2,128)(2,1)}, u32[]{:S(2)}) copy-start(bf16[2,4096]{1,0:T(2,128)(2,1)} %queries_ref.3) | copy-start | bytes 49156
  9.1 7.4 %copy-start.1 = (bf16[2,2,512]{2,1,0:T(2,128)(2,1)S(1)}, bf16[2,2,512]{2,1,0:T(2,128)(2,1)}, u32[]{:S(2)}) copy-start(bf16[2,2,512]{2,1,0:T(2,128)(2,1)} %fresh_ref.1) | copy-start | bytes 12292

commit v10 on v9

--- a/solution.py
+++ b/solution.py
@@ -38,13 +38,35 @@
     return [pl.BlockSpec(memory_space=VMEM)] * n
 
 
-def send_kernel(slots, pages, page_ref, lengths_ref, queries_ref, table_ref, out_ref):
-    peers = out_ref.shape[0]
+def send_kernel(
+    slots, pages, page_ref, lengths_ref, queries_ref, table_ref, out_hbm, out_ref, sems
+):
+    peers = out_hbm.shape[0]
     own_rows, most_pages = table_ref.shape
     heads = queries_ref.shape[1] // HEAD_SIZE
     page_tok = 16
     slot_bits = slots.bit_length() - 1
     page_bits = pages.bit_length() - 1
+    sub = lax.broadcasted_iota(jnp.int32, (8, HEAD_SIZE), 0)
+    pieces = []
+    for g in range(heads // 8):
+        pair = [jnp.zeros((8, HEAD_SIZE), f32)] * own_rows
+        for head in range(8):
+            at = (g * 8 + head) * HEAD_SIZE
+            both = queries_ref[:, at : at + HEAD_SIZE].astype(f32)
+            pair = [
+                jnp.where(sub == head, both[row : row + 1, :], pair[row]) for row in range(own_rows)
+            ]
+        pieces += pair
+    queries = jnp.concatenate(pieces, axis=0).astype(bf16)
+    rows = own_rows * heads
+    for peer in range(peers):
+        out_ref[peer, 0:rows, :] = queries
+    stores = [
+        pltpu.make_async_copy(out_ref.at[:, at], out_hbm.at[:, at], sems.at[n])
+        for n, at in enumerate((pl.ds(0, rows), pl.ds(rows, 8)))
+    ]
+    stores[0].start()
     column = lax.broadcasted_iota(jnp.int32, (1, most_pages), 1)
     lender_rows = lax.broadcasted_iota(jnp.int32, (peers, most_pages), 0)
     slot_rows = lax.broadcasted_iota(jnp.int32, (slots, most_pages), 0)
@@ -58,26 +80,15 @@
         a = jnp.where(lender_rows == lender, fill.astype(f32), 0.0).astype(bf16)
         b = jnp.where(slot_rows == slot, 1.0, 0.0).astype(bf16)
         fills.append(nt_dot(a, b))
-    sub = lax.broadcasted_iota(jnp.int32, (8, HEAD_SIZE), 0)
-    pieces = []
-    for g in range(heads // 8):
-        pair = [jnp.zeros((8, HEAD_SIZE), f32)] * own_rows
-        for head in range(8):
-            at = (g * 8 + head) * HEAD_SIZE
-            both = queries_ref[:, at : at + HEAD_SIZE].astype(f32)
-            pair = [
-                jnp.where(sub == head, both[row : row + 1, :], pair[row]) for row in range(own_rows)
-            ]
-        pieces += pair
-    queries = jnp.concatenate(pieces, axis=0).astype(bf16)
-    rows = own_rows * heads
     sub = lax.broadcasted_iota(jnp.int32, (8, slots), 0)
     for peer in range(peers):
-        out_ref[peer, 0:rows, :] = queries
         tile = jnp.zeros((8, slots), f32)
         for row in range(own_rows):
             tile = jnp.where(sub == row, fills[row][peer : peer + 1, :], tile)
         out_ref[peer, rows : rows + 8, :] = tile.astype(bf16)
+    stores[1].start()
+    for store in stores:
+        store.wait()
 
 
 def new_token(queries_ref, fresh_ref, token_ref):
@@ -196,7 +207,6 @@
 
     lax.fori_loop(0, page_tok, score_step, 0, unroll=8)
 
-    load.wait()
     new_token(queries_ref, fresh_ref, token_ref)
     owner_h = jnp.broadcast_to(owner[0:1], (heads, slots))
     fill_h = jnp.broadcast_to(fill[0:1], (heads, slots))
@@ -222,6 +232,7 @@
         high = scaled.astype(bf16).astype(f32)
         score_ref[t] = high
         weight_ref[t] = scaled - high
+    load.wait()
     page_sum = page_sum * factor
     masks = [
         jnp.where(owner_16 == (2 * k + 1 + sub16 // 8).astype(f32), 1.0, 0.0).astype(bf16)
@@ -363,7 +374,11 @@
         functools.partial(send_kernel, slots, pages),
         out_shape=jax.ShapeDtypeStruct((lenders, rows + 8, HEAD_SIZE), bf16),
         in_specs=[pl.BlockSpec(memory_space=SMEM)] * 2 + vmem_specs(2),
-        out_specs=pl.BlockSpec(memory_space=VMEM),
+        out_specs=pl.BlockSpec(memory_space=pl.ANY),
+        scratch_shapes=[
+            pltpu.VMEM((lenders, rows + 8, HEAD_SIZE), bf16),
+            pltpu.SemaphoreType.DMA((2,)),
+        ],
         name="send",
     )(page_index, lengths, queries, block_table)
     received = lax.all_to_all(to_send, "inst", 0, 0)

time: 52 us -> 51.9 us (level)
  no operation moved by 1% of the time
where the time goes in v10:
time: 51.9 us; the launch traced here: 51.6 us
  blocking collectives  29.5 us (57%)
  Pallas kernels  10.4 us (20%)
  starting transfers between devices  7.4 us (14%)
  waiting for transfers between devices  4.19 us (8%)
    all_to_all x1, blocking collectives, shards(): page_parts = lax.all_to_all(combined, 'page', 0, 0)  17.5 us
    all_to_all x1, blocking collectives, shards(): parts = lax.all_to_all(partial, 'inst', 0, 0)  12 us
    all_to_all x1, starting transfers between devices, shards(): received = lax.all_to_all(to_send, 'inst', 0, 0)  7.4 us
    pallas_call x1, Pallas kernels, shards(): pl.pallas_call(attend_kernel, out_shape=(jax.ShapeDtypeStruct((lenders, r...  4.23 us
    all_to_all x1, waiting for transfers between devices, shards(): received = lax.all_to_all(to_send, 'inst', 0, 0)  4.19 us
    pallas_call x1, Pallas kernels, shards(): pl.pallas_call(token_major_kernel, out_shape=(jax.ShapeDtypeStruct((page_...  3.16 us
    pallas_call x1, Pallas kernels, shards(): pl.pallas_call(functools.partial(send_kernel, slots, pages), out_shape=ja...  1.65 us
  transfers between devices with their start and end apart: 1, of which 1 were waited for; matrix products, arithmetic and copies ran while one was open for 0% of the time, Pallas kernels for 6%

profile of v10, /device:TPU:8, one launch (start us, length us, event | category | flops | bytes accessed | tf_op | source)
XLA Modules:
  0.0 51.6 jit_solution(17459070880818778455)
XLA Ops:
  0.0 1.6 %send.1 = bf16[16,72,128]{2,1,0:T(8,128)(2,1)} custom-call(s32[1]{0:T(128)} %bitcast.page_ref, s32[2]{0:T(128)} %lengths_ref.1, bf16[2,4096]{1,0:T(2,128)(2,1)} %queries_ref.3, s32[2,768]{1,0:T(2,128)} %table_ref.1), custom_call_target="tpu_custom_call" | custom-call | tf_op jit(solution)/shard_map/send/pallas_call | solution.py:373
  1.7 7.4 %all-to-all-start = ((bf16[16,72,128]{2,1,0:T(8,128)(2,1)}), bf16[16,72,128]{2,1,0:T(8,128)(2,1)S(1)}, u32[]{:S(2)}, u32[]{:S(2)}) async-start(bf16[16,72,128]{2,1,0:T(8,128)(2,1)} %send.1), calls=%async_computation | async-start | bytes 589824 | tf_op jit(solution)/shard_map/all_to_all | solution.py:384
  9.1 0.0 copy-start
  9.1 0.0 copy-start.1
  9.1 3.2 %token_major.1 = (bf16[16,128,512]{2,1,0:T(8,128)(2,1)S(1)}, bf16[16,128,512]{2,1,0:T(8,128)(2,1)}) custom-call(bf16[2,128,16,512]{3,2,1,0:T(8,128)(2,1)} %pool_hbm.1), custom_call_target="tpu_custom_call" | custom-call | flops 1000000000 | bytes 8388608 | tf_op jit(solution)/shard_map/token_major/pallas_call | solution.py:386
  12.2 4.2 %all-to-all-done.recv_ref = bf16[16,72,128]{2,1,0:T(8,128)(2,1)S(1)} async-done(((bf16[16,72,128]{2,1,0:T(8,128)(2,1)}), bf16[16,72,128]{2,1,0:T(8,128)(2,1)S(1)}, u32[]{:S(2)}, u32[]{:S(2)}) %all-to-all-start) | async-done | bytes 294944 | tf_op jit(solution)/shard_map/all_to_all | solution.py:384
  16.4 0.0 copy-done
  16.4 0.0 copy-done.1
  16.4 4.2 %attend.1 = (s16[16,72,128]{2,1,0:T(8,128)(2,1)S(1)}, f32[16,128]{1,0:T(8,128)S(1)}) custom-call(bf16[16,72,128]{2,1,0:T(8,128)(2,1)S(1)} %all-to-all-done.recv_ref, bf16[16,128,512]{2,1,0:T(8,128)(2,1)S(1)} %get-tuple-element.9.keys_ref, bf16[2,4096]{1,0:T(2,128)(2,1)S(1)} %copy-done, bf16[2,2,512]{2,1,0:T(2,128)(2,1)S(1)} %copy-done.1, ...), custom_call_target="tpu_custom_call" | custom-call | tf_op jit(solution)/shard_map/attend/pallas_call | solution.py:405
  20.7 12.0 %all_to_all.15.parts_ref = s16[16,72,128]{2,1,0:T(8,128)(2,1)S(1)} all-to-all(s16[16,72,128]{2,1,0:T(8,128)(2,1)S(1)} %get-tuple-element.11), channel_id=1, replica_groups=mesh['inst'=16,'page'=8,'head'=2] {'inst'}, dimensions={0} | all-to-all | bytes 589824 | tf_op jit(solution)/shard_map/all_to_all | solution.py:422
  32.7 0.5 combine.1
  33.2 17.5 %all_to_all.16.parts_ref = s16[8,72,128]{2,1,0:T(8,128)(2,1)S(1)} all-to-all(s16[8,72,128]{2,1,0:T(8,128)(2,1)S(1)} %combine.1), channel_id=1, replica_groups=mesh['inst'=16,'page'=8,'head'=2] {'page'}, dimensions={0} | all-to-all | bytes 294912 | tf_op jit(solution)/shard_map/all_to_all | solution.py:432
  50.7 0.9 %finish.1 = bf16[2,4096]{1,0:T(2,128)(2,1)} custom-call(s16[8,72,128]{2,1,0:T(8,128)(2,1)S(1)} %all_to_all.16.parts_ref, f32[16,128]{1,0:T(8,128)S(1)} %get-tuple-element.12.token_ref), custom_call_target="tpu_custom_call" | custom-call | tf_op jit(solution)/shard_map/finish/pallas_call | solution.py:434
Async XLA Ops:
  1.7 14.8 %all-to-all-start = ((bf16[16,72,128]{2,1,0:T(8,128)(2,1)}), bf16[16,72,128]{2,1,0:T(8,128)(2,1)S(1)}, u32[]{:S(2)}, u32[]{:S(2)}) async-start(bf16[16,72,128]{2,1,0:T(8,128)(2,1)} %send.1), calls=%async_computation | async-start | bytes 589824 | tf_op jit(solution)/shard_map/all_to_all | solution.py:384
  9.1 7.4 %copy-start = (bf16[2,4096]{1,0:T(2,128)(2,1)S(1)}, bf16[2,4096]{1,0:T(2,128)(2,1)}, u32[]{:S(2)}) copy-start(bf16[2,4096]{1,0:T(2,128)(2,1)} %queries_ref.3) | copy-start | bytes 49156
  9.1 7.4 %copy-start.1 = (bf16[2,2,512]{2,1,0:T(2,128)(2,1)S(1)}, bf16[2,2,512]{2,1,0:T(2,128)(2,1)}, u32[]{:S(2)}) copy-start(bf16[2,2,512]{2,1,0:T(2,128)(2,1)} %fresh_ref.1) | copy-start | bytes 12292

commit v11 on v10

--- a/solution.py
+++ b/solution.py
@@ -173,12 +173,20 @@
     values_ref,
     score_ref,
     weight_ref,
-    sem,
+    sems,
 ):
     peers = recv_ref.shape[0]
     page_tok, slots, width = keys_ref.shape
-    load = pltpu.make_async_copy(values_hbm, values_ref, sem)
-    load.start()
+
+    def load(i):
+        at = pl.ds(i * (page_tok // 2), page_tok // 2)
+        return pltpu.make_async_copy(values_hbm.at[at], values_ref.at[at], sems.at[i])
+
+    def load_step(i, carry):
+        load(i).start()
+        return carry
+
+    lax.fori_loop(0, 2, load_step, 0)
     groups = width // HEAD_SIZE
     requests = 2 * peers
     heads = groups * 8
@@ -205,7 +213,7 @@
             score_ref[t, g * 8 : (g + 1) * 8, :] = jnp.where(live, picked * SCALE, LOWEST_SCORE)
         return carry
 
-    lax.fori_loop(0, page_tok, score_step, 0, unroll=8)
+    lax.fori_loop(0, page_tok, score_step, 0, unroll=True)
 
     new_token(queries_ref, fresh_ref, token_ref)
     owner_h = jnp.broadcast_to(owner[0:1], (heads, slots))
@@ -232,7 +240,8 @@
         high = scaled.astype(bf16).astype(f32)
         score_ref[t] = high
         weight_ref[t] = scaled - high
-    load.wait()
+    for i in range(2):
+        load(i).wait()
     page_sum = page_sum * factor
     masks = [
         jnp.where(owner_16 == (2 * k + 1 + sub16 // 8).astype(f32), 1.0, 0.0).astype(bf16)
@@ -414,7 +423,7 @@
             pltpu.VMEM(values.shape, bf16),
             pltpu.VMEM((page_tok, groups * 8, slots), f32),
             pltpu.VMEM((page_tok, groups * 8, slots), f32),
-            pltpu.SemaphoreType.DMA,
+            pltpu.SemaphoreType.DMA((2,)),
         ],
         compiler_params=pltpu.CompilerParams(vmem_limit_bytes=51 * 2**20),
         name="attend",

time: 51.9 us -> 51.7 us (level)
  no operation moved by 1% of the time
where the time goes in v11:
time: 51.7 us; the launch traced here: 51.4 us
  blocking collectives  29.5 us (57%)
  Pallas kernels  10.2 us (20%)
  starting transfers between devices  7.4 us (14%)
  waiting for transfers between devices  4.19 us (8%)
    all_to_all x1, blocking collectives, shards(): page_parts = lax.all_to_all(combined, 'page', 0, 0)  17.5 us
    all_to_all x1, blocking collectives, shards(): parts = lax.all_to_all(partial, 'inst', 0, 0)  12 us
    all_to_all x1, starting transfers between devices, shards(): received = lax.all_to_all(to_send, 'inst', 0, 0)  7.4 us
    all_to_all x1, waiting for transfers between devices, shards(): received = lax.all_to_all(to_send, 'inst', 0, 0)  4.19 us
    pallas_call x1, Pallas kernels, shards(): pl.pallas_call(attend_kernel, out_shape=(jax.ShapeDtypeStruct((lenders, r...  4 us
    pallas_call x1, Pallas kernels, shards(): pl.pallas_call(token_major_kernel, out_shape=(jax.ShapeDtypeStruct((page_...  3.16 us
    pallas_call x1, Pallas kernels, shards(): pl.pallas_call(functools.partial(send_kernel, slots, pages), out_shape=ja...  1.65 us
  transfers between devices with their start and end apart: 1, of which 1 were waited for; matrix products, arithmetic and copies ran while one was open for 0% of the time, Pallas kernels for 6%

profile of v11, /device:TPU:8, one launch (start us, length us, event | category | flops | bytes accessed | tf_op | source)
XLA Modules:
  0.0 51.4 jit_solution(15551174582744938792)
XLA Ops:
  0.0 1.6 %send.1 = bf16[16,72,128]{2,1,0:T(8,128)(2,1)} custom-call(s32[1]{0:T(128)} %bitcast.page_ref, s32[2]{0:T(128)} %lengths_ref.1, bf16[2,4096]{1,0:T(2,128)(2,1)} %queries_ref.3, s32[2,768]{1,0:T(2,128)} %table_ref.1), custom_call_target="tpu_custom_call" | custom-call | tf_op jit(solution)/shard_map/send/pallas_call | solution.py:382
  1.7 7.4 %all-to-all-start = ((bf16[16,72,128]{2,1,0:T(8,128)(2,1)}), bf16[16,72,128]{2,1,0:T(8,128)(2,1)S(1)}, u32[]{:S(2)}, u32[]{:S(2)}) async-start(bf16[16,72,128]{2,1,0:T(8,128)(2,1)} %send.1), calls=%async_computation | async-start | bytes 589824 | tf_op jit(solution)/shard_map/all_to_all | solution.py:393
  9.1 0.0 copy-start
  9.1 0.0 copy-start.1
  9.1 3.2 %token_major.1 = (bf16[16,128,512]{2,1,0:T(8,128)(2,1)S(1)}, bf16[16,128,512]{2,1,0:T(8,128)(2,1)}) custom-call(bf16[2,128,16,512]{3,2,1,0:T(8,128)(2,1)} %pool_hbm.1), custom_call_target="tpu_custom_call" | custom-call | flops 1000000000 | bytes 8388608 | tf_op jit(solution)/shard_map/token_major/pallas_call | solution.py:395
  12.2 4.2 %all-to-all-done.recv_ref = bf16[16,72,128]{2,1,0:T(8,128)(2,1)S(1)} async-done(((bf16[16,72,128]{2,1,0:T(8,128)(2,1)}), bf16[16,72,128]{2,1,0:T(8,128)(2,1)S(1)}, u32[]{:S(2)}, u32[]{:S(2)}) %all-to-all-start) | async-done | bytes 294944 | tf_op jit(solution)/shard_map/all_to_all | solution.py:393
  16.4 0.0 copy-done
  16.4 0.0 copy-done.1
  16.4 4.0 %attend.1 = (s16[16,72,128]{2,1,0:T(8,128)(2,1)S(1)}, f32[16,128]{1,0:T(8,128)S(1)}) custom-call(bf16[16,72,128]{2,1,0:T(8,128)(2,1)S(1)} %all-to-all-done.recv_ref, bf16[16,128,512]{2,1,0:T(8,128)(2,1)S(1)} %get-tuple-element.9.keys_ref, bf16[2,4096]{1,0:T(2,128)(2,1)S(1)} %copy-done, bf16[2,2,512]{2,1,0:T(2,128)(2,1)S(1)} %copy-done.1, ...), custom_call_target="tpu_custom_call" | custom-call | tf_op jit(solution)/shard_map/attend/pallas_call | solution.py:414
  20.4 12.0 %all_to_all.15.parts_ref = s16[16,72,128]{2,1,0:T(8,128)(2,1)S(1)} all-to-all(s16[16,72,128]{2,1,0:T(8,128)(2,1)S(1)} %get-tuple-element.11), channel_id=1, replica_groups=mesh['inst'=16,'page'=8,'head'=2] {'inst'}, dimensions={0} | all-to-all | bytes 589824 | tf_op jit(solution)/shard_map/all_to_all | solution.py:431
  32.5 0.5 combine.1
  32.9 17.5 %all_to_all.16.parts_ref = s16[8,72,128]{2,1,0:T(8,128)(2,1)S(1)} all-to-all(s16[8,72,128]{2,1,0:T(8,128)(2,1)S(1)} %combine.1), channel_id=1, replica_groups=mesh['inst'=16,'page'=8,'head'=2] {'page'}, dimensions={0} | all-to-all | bytes 294912 | tf_op jit(solution)/shard_map/all_to_all | solution.py:441
  50.5 0.9 %finish.1 = bf16[2,4096]{1,0:T(2,128)(2,1)} custom-call(s16[8,72,128]{2,1,0:T(8,128)(2,1)S(1)} %all_to_all.16.parts_ref, f32[16,128]{1,0:T(8,128)S(1)} %get-tuple-element.12.token_ref), custom_call_target="tpu_custom_call" | custom-call | tf_op jit(solution)/shard_map/finish/pallas_call | solution.py:443
Async XLA Ops:
  1.7 14.8 %all-to-all-start = ((bf16[16,72,128]{2,1,0:T(8,128)(2,1)}), bf16[16,72,128]{2,1,0:T(8,128)(2,1)S(1)}, u32[]{:S(2)}, u32[]{:S(2)}) async-start(bf16[16,72,128]{2,1,0:T(8,128)(2,1)} %send.1), calls=%async_computation | async-start | bytes 589824 | tf_op jit(solution)/shard_map/all_to_all | solution.py:393
  9.1 7.4 %copy-start = (bf16[2,4096]{1,0:T(2,128)(2,1)S(1)}, bf16[2,4096]{1,0:T(2,128)(2,1)}, u32[]{:S(2)}) copy-start(bf16[2,4096]{1,0:T(2,128)(2,1)} %queries_ref.3) | copy-start | bytes 49156
  9.1 7.4 %copy-start.1 = (bf16[2,2,512]{2,1,0:T(2,128)(2,1)S(1)}, bf16[2,2,512]{2,1,0:T(2,128)(2,1)}, u32[]{:S(2)}) copy-start(bf16[2,2,512]{2,1,0:T(2,128)(2,1)} %fresh_ref.1) | copy-start | bytes 12292

commit v12 on v11

--- a/solution.py
+++ b/solution.py
@@ -251,6 +251,14 @@
         jnp.sum(jnp.where(owner_h == float(r + 1), page_sum, 0.0), axis=1, keepdims=True)
         for r in range(requests)
     ]
+    heads_of_stats = []
+    for peer in range(peers):
+        columns = []
+        for g in range(groups):
+            at = slice(g * 8, (g + 1) * 8)
+            for r in (2 * peer, 2 * peer + 1):
+                columns.append((maxima[r][at], totals[r][at]))
+        heads_of_stats.append(stat_head(columns, LENDER_UNIT))
     scales = []
     for g in range(groups):
         acc = jnp.zeros((requests * 8, HEAD_SIZE), f32)
@@ -271,34 +279,36 @@
         scales.append(k)
         out_ref[:, g * 16 : (g + 1) * 16, :] = code.reshape(peers, 16, HEAD_SIZE)
     for peer in range(peers):
-        columns = []
-        for g in range(groups):
-            for row in range(2):
-                r = 2 * peer + row
-                at = slice(g * 8, (g + 1) * 8)
-                columns.append((maxima[r][at], totals[r][at], scales[g][r * 8 : (r + 1) * 8]))
-        out_ref[peer, rows : rows + 8, :] = stat_tile(columns, LENDER_UNIT)
+        columns = [
+            scales[g][r * 8 : (r + 1) * 8]
+            for g in range(groups)
+            for r in (2 * peer, 2 * peer + 1)
+        ]
+        out_ref[peer, rows : rows + 8, :] = stat_tile(heads_of_stats[peer], columns)
 
 
 LENDER_UNIT = 8.0
 OWNER_UNIT = 1.0
 
 
-def stat_tile(columns, unit):
+def stat_head(columns, unit):
     tiles = len(columns)
     lane = lax.broadcasted_iota(jnp.int32, (8, HEAD_SIZE), 1)
     top = jnp.zeros((8, HEAD_SIZE), f32)
     total = top
-    scale = top
-    for c, (m, l, k) in enumerate(columns):
+    for c, (m, l) in enumerate(columns):
         top = jnp.where(lane == c, m, top)
         total = jnp.where((lane == tiles + c) | (lane == 2 * tiles + c), l, total)
-        scale = jnp.where(lane == 3 * tiles + c, k, scale)
     total = total * unit
     whole = jnp.floor(total)
     part = jnp.round((total - whole) * PART)
-    tile = jnp.where(lane < tiles, top, jnp.where(lane < 2 * tiles, whole, part))
-    tile = jnp.where(lane < 3 * tiles, tile, scale)
+    return jnp.where(lane < tiles, top, jnp.where(lane < 2 * tiles, whole, part))
+
+
+def stat_tile(tile, scales):
+    lane = lax.broadcasted_iota(jnp.int32, (8, HEAD_SIZE), 1)
+    for c, k in enumerate(scales):
+        tile = jnp.where(lane == 3 * len(scales) + c, k, tile)
     return tile.astype(jnp.int32).astype(jnp.int16)
 
 
@@ -336,11 +346,12 @@
     tiles = 2 * groups
     top, total, sums = merge(parts_ref, groups, LENDER_UNIT)
     coded = [encode_rows(jnp.concatenate(sums[2 * g : 2 * g + 2], axis=0)) for g in range(groups)]
-    columns = [
-        (top[:, c : c + 1], total[:, c : c + 1], coded[c // 2][0][c % 2 * 8 : c % 2 * 8 + 8])
-        for c in range(tiles)
-    ]
-    stat = stat_tile(columns, OWNER_UNIT)
+    head = stat_head(
+        [(top[:, c : c + 1], total[:, c : c + 1]) for c in range(tiles)], OWNER_UNIT
+    )
+    stat = stat_tile(
+        head, [coded[c // 2][0][c % 2 * 8 : c % 2 * 8 + 8] for c in range(tiles)]
+    )
     for i in range(out_ref.shape[0]):
         for g in range(groups):
             out_ref[i, g * 16 : (g + 1) * 16, :] = coded[g][1]

time: 51.7 us -> 51.7 us (level)
  no operation moved by 1% of the time
where the time goes in v12:
time: 51.7 us; the launch traced here: 51.4 us
  blocking collectives  29.5 us (57%)
  Pallas kernels  10.2 us (20%)
  starting transfers between devices  7.4 us (14%)
  waiting for transfers between devices  4.19 us (8%)
    all_to_all x1, blocking collectives, shards(): page_parts = lax.all_to_all(combined, 'page', 0, 0)  17.5 us
    all_to_all x1, blocking collectives, shards(): parts = lax.all_to_all(partial, 'inst', 0, 0)  12 us
    all_to_all x1, starting transfers between devices, shards(): received = lax.all_to_all(to_send, 'inst', 0, 0)  7.4 us
    all_to_all x1, waiting for transfers between devices, shards(): received = lax.all_to_all(to_send, 'inst', 0, 0)  4.19 us
    pallas_call x1, Pallas kernels, shards(): pl.pallas_call(attend_kernel, out_shape=(jax.ShapeDtypeStruct((lenders, r...  4 us
    pallas_call x1, Pallas kernels, shards(): pl.pallas_call(token_major_kernel, out_shape=(jax.ShapeDtypeStruct((page_...  3.16 us
    pallas_call x1, Pallas kernels, shards(): pl.pallas_call(functools.partial(send_kernel, slots, pages), out_shape=ja...  1.65 us
  transfers between devices with their start and end apart: 1, of which 1 were waited for; matrix products, arithmetic and copies ran while one was open for 0% of the time, Pallas kernels for 6%

profile of v12, /device:TPU:8, one launch (start us, length us, event | category | flops | bytes accessed | tf_op | source)
XLA Modules:
  0.0 51.4 jit_solution(14594698355779377116)
XLA Ops:
  0.0 1.6 %send.1 = bf16[16,72,128]{2,1,0:T(8,128)(2,1)} custom-call(s32[1]{0:T(128)} %bitcast.page_ref, s32[2]{0:T(128)} %lengths_ref.1, bf16[2,4096]{1,0:T(2,128)(2,1)} %queries_ref.3, s32[2,768]{1,0:T(2,128)} %table_ref.1), custom_call_target="tpu_custom_call" | custom-call | tf_op jit(solution)/shard_map/send/pallas_call | solution.py:393
  1.7 7.4 %all-to-all-start = ((bf16[16,72,128]{2,1,0:T(8,128)(2,1)}), bf16[16,72,128]{2,1,0:T(8,128)(2,1)S(1)}, u32[]{:S(2)}, u32[]{:S(2)}) async-start(bf16[16,72,128]{2,1,0:T(8,128)(2,1)} %send.1), calls=%async_computation | async-start | bytes 589824 | tf_op jit(solution)/shard_map/all_to_all | solution.py:404
  9.1 0.0 copy-start
  9.1 0.0 copy-start.1
  9.1 3.2 %token_major.1 = (bf16[16,128,512]{2,1,0:T(8,128)(2,1)S(1)}, bf16[16,128,512]{2,1,0:T(8,128)(2,1)}) custom-call(bf16[2,128,16,512]{3,2,1,0:T(8,128)(2,1)} %pool_hbm.1), custom_call_target="tpu_custom_call" | custom-call | flops 1000000000 | bytes 8388608 | tf_op jit(solution)/shard_map/token_major/pallas_call | solution.py:406
  12.2 4.2 %all-to-all-done.recv_ref = bf16[16,72,128]{2,1,0:T(8,128)(2,1)S(1)} async-done(((bf16[16,72,128]{2,1,0:T(8,128)(2,1)}), bf16[16,72,128]{2,1,0:T(8,128)(2,1)S(1)}, u32[]{:S(2)}, u32[]{:S(2)}) %all-to-all-start) | async-done | bytes 294944 | tf_op jit(solution)/shard_map/all_to_all | solution.py:404
  16.4 0.0 copy-done
  16.4 0.0 copy-done.1
  16.4 4.0 %attend.1 = (s16[16,72,128]{2,1,0:T(8,128)(2,1)S(1)}, f32[16,128]{1,0:T(8,128)S(1)}) custom-call(bf16[16,72,128]{2,1,0:T(8,128)(2,1)S(1)} %all-to-all-done.recv_ref, bf16[16,128,512]{2,1,0:T(8,128)(2,1)S(1)} %get-tuple-element.9.keys_ref, bf16[2,4096]{1,0:T(2,128)(2,1)S(1)} %copy-done, bf16[2,2,512]{2,1,0:T(2,128)(2,1)S(1)} %copy-done.1, ...), custom_call_target="tpu_custom_call" | custom-call | tf_op jit(solution)/shard_map/attend/pallas_call | solution.py:425
  20.4 12.0 %all_to_all.15.parts_ref = s16[16,72,128]{2,1,0:T(8,128)(2,1)S(1)} all-to-all(s16[16,72,128]{2,1,0:T(8,128)(2,1)S(1)} %get-tuple-element.11), channel_id=1, replica_groups=mesh['inst'=16,'page'=8,'head'=2] {'inst'}, dimensions={0} | all-to-all | bytes 589824 | tf_op jit(solution)/shard_map/all_to_all | solution.py:442
  32.5 0.5 combine.1
  32.9 17.5 %all_to_all.16.parts_ref = s16[8,72,128]{2,1,0:T(8,128)(2,1)S(1)} all-to-all(s16[8,72,128]{2,1,0:T(8,128)(2,1)S(1)} %combine.1), channel_id=1, replica_groups=mesh['inst'=16,'page'=8,'head'=2] {'page'}, dimensions={0} | all-to-all | bytes 294912 | tf_op jit(solution)/shard_map/all_to_all | solution.py:452
  50.5 0.9 %finish.1 = bf16[2,4096]{1,0:T(2,128)(2,1)} custom-call(s16[8,72,128]{2,1,0:T(8,128)(2,1)S(1)} %all_to_all.16.parts_ref, f32[16,128]{1,0:T(8,128)S(1)} %get-tuple-element.12.token_ref), custom_call_target="tpu_custom_call" | custom-call | tf_op jit(solution)/shard_map/finish/pallas_call | solution.py:454
Async XLA Ops:
  1.7 14.8 %all-to-all-start = ((bf16[16,72,128]{2,1,0:T(8,128)(2,1)}), bf16[16,72,128]{2,1,0:T(8,128)(2,1)S(1)}, u32[]{:S(2)}, u32[]{:S(2)}) async-start(bf16[16,72,128]{2,1,0:T(8,128)(2,1)} %send.1), calls=%async_computation | async-start | bytes 589824 | tf_op jit(solution)/shard_map/all_to_all | solution.py:404
  9.1 7.4 %copy-start = (bf16[2,4096]{1,0:T(2,128)(2,1)S(1)}, bf16[2,4096]{1,0:T(2,128)(2,1)}, u32[]{:S(2)}) copy-start(bf16[2,4096]{1,0:T(2,128)(2,1)} %queries_ref.3) | copy-start | bytes 49156
  9.1 7.4 %copy-start.1 = (bf16[2,2,512]{2,1,0:T(2,128)(2,1)S(1)}, bf16[2,2,512]{2,1,0:T(2,128)(2,1)}, u32[]{:S(2)}) copy-start(bf16[2,2,512]{2,1,0:T(2,128)(2,1)} %fresh_ref.1) | copy-start | bytes 12292

commit v13 on v11

--- a/solution.py
+++ b/solution.py
@@ -39,7 +39,7 @@
 
 
 def send_kernel(
-    slots, pages, page_ref, lengths_ref, queries_ref, table_ref, out_hbm, out_ref, sems
+    slots, pages, lengths_ref, queries_ref, table_ref, out_hbm, out_ref, sems
 ):
     peers = out_hbm.shape[0]
     own_rows, most_pages = table_ref.shape
@@ -74,7 +74,7 @@
     for row in range(own_rows):
         entry = table_ref[row : row + 1, :]
         fill = jnp.clip(lengths_ref[row] - column * page_tok, 0, page_tok)
-        here = ((entry >> slot_bits) & (pages - 1)) == page_ref[0]
+        here = ((entry >> slot_bits) & (pages - 1)) == lax.axis_index("page")
         lender = jnp.where(here & (entry >= 0), entry >> (slot_bits + page_bits), -1)
         slot = entry & (slots - 1)
         a = jnp.where(lender_rows == lender, fill.astype(f32), 0.0).astype(bf16)
@@ -377,19 +377,18 @@
     slots, page_tok, width = key_value_pool.shape[1:]
     groups = width // HEAD_SIZE
     rows = groups * 16
-    page_index = lax.axis_index("page").reshape(1).astype(jnp.int32)
 
     to_send = pl.pallas_call(
         functools.partial(send_kernel, slots, pages),
         out_shape=jax.ShapeDtypeStruct((lenders, rows + 8, HEAD_SIZE), bf16),
-        in_specs=[pl.BlockSpec(memory_space=SMEM)] * 2 + vmem_specs(2),
+        in_specs=[pl.BlockSpec(memory_space=SMEM)] + vmem_specs(2),
         out_specs=pl.BlockSpec(memory_space=pl.ANY),
         scratch_shapes=[
             pltpu.VMEM((lenders, rows + 8, HEAD_SIZE), bf16),
             pltpu.SemaphoreType.DMA((2,)),
         ],
         name="send",
-    )(page_index, lengths, queries, block_table)
+    )(lengths, queries, block_table)
     received = lax.all_to_all(to_send, "inst", 0, 0)
 
     keys, values = pl.pallas_call(

time: 51.7 us -> 51.7 us (level)
  no operation moved by 1% of the time
where the time goes in v13:
time: 51.7 us; the launch traced here: 51.4 us
  blocking collectives  29.5 us (57%)
  Pallas kernels  10.2 us (20%)
  starting transfers between devices  7.4 us (14%)
  waiting for transfers between devices  4.19 us (8%)
    all_to_all x1, blocking collectives, shards(): page_parts = lax.all_to_all(combined, 'page', 0, 0)  17.5 us
    all_to_all x1, blocking collectives, shards(): parts = lax.all_to_all(partial, 'inst', 0, 0)  12 us
    all_to_all x1, starting transfers between devices, shards(): received = lax.all_to_all(to_send, 'inst', 0, 0)  7.4 us
    all_to_all x1, waiting for transfers between devices, shards(): received = lax.all_to_all(to_send, 'inst', 0, 0)  4.19 us
    pallas_call x1, Pallas kernels, shards(): pl.pallas_call(attend_kernel, out_shape=(jax.ShapeDtypeStruct((lenders, r...  4 us
    pallas_call x1, Pallas kernels, shards(): pl.pallas_call(token_major_kernel, out_shape=(jax.ShapeDtypeStruct((page_...  3.16 us
    pallas_call x1, Pallas kernels, shards(): pl.pallas_call(functools.partial(send_kernel, slots, pages), out_shape=ja...  1.65 us
  transfers between devices with their start and end apart: 1, of which 1 were waited for; matrix products, arithmetic and copies ran while one was open for 0% of the time, Pallas kernels for 6%

profile of v13, /device:TPU:8, one launch (start us, length us, event | category | flops | bytes accessed | tf_op | source)
XLA Modules:
  0.0 51.4 jit_solution(10804747810980555835)
XLA Ops:
  0.0 1.6 %send.1 = bf16[16,72,128]{2,1,0:T(8,128)(2,1)} custom-call(s32[2]{0:T(128)} %lengths_ref.1, bf16[2,4096]{1,0:T(2,128)(2,1)} %queries_ref.3, s32[2,768]{1,0:T(2,128)} %table_ref.1), custom_call_target="tpu_custom_call" | custom-call | tf_op jit(solution)/shard_map/send/pallas_call | solution.py:381
  1.7 7.4 %all-to-all-start = ((bf16[16,72,128]{2,1,0:T(8,128)(2,1)}), bf16[16,72,128]{2,1,0:T(8,128)(2,1)S(1)}, u32[]{:S(2)}, u32[]{:S(2)}) async-start(bf16[16,72,128]{2,1,0:T(8,128)(2,1)} %send.1), calls=%async_computation | async-start | bytes 589824 | tf_op jit(solution)/shard_map/all_to_all | solution.py:392
  9.1 0.0 copy-start
  9.1 0.0 copy-start.1
  9.1 3.2 %token_major.1 = (bf16[16,128,512]{2,1,0:T(8,128)(2,1)S(1)}, bf16[16,128,512]{2,1,0:T(8,128)(2,1)}) custom-call(bf16[2,128,16,512]{3,2,1,0:T(8,128)(2,1)} %pool_hbm.1), custom_call_target="tpu_custom_call" | custom-call | flops 1000000000 | bytes 8388608 | tf_op jit(solution)/shard_map/token_major/pallas_call | solution.py:394
  12.2 4.2 %all-to-all-done.recv_ref = bf16[16,72,128]{2,1,0:T(8,128)(2,1)S(1)} async-done(((bf16[16,72,128]{2,1,0:T(8,128)(2,1)}), bf16[16,72,128]{2,1,0:T(8,128)(2,1)S(1)}, u32[]{:S(2)}, u32[]{:S(2)}) %all-to-all-start) | async-done | bytes 294944 | tf_op jit(solution)/shard_map/all_to_all | solution.py:392
  16.4 0.0 copy-done
  16.4 0.0 copy-done.1
  16.4 4.0 %attend.1 = (s16[16,72,128]{2,1,0:T(8,128)(2,1)S(1)}, f32[16,128]{1,0:T(8,128)S(1)}) custom-call(bf16[16,72,128]{2,1,0:T(8,128)(2,1)S(1)} %all-to-all-done.recv_ref, bf16[16,128,512]{2,1,0:T(8,128)(2,1)S(1)} %get-tuple-element.9.keys_ref, bf16[2,4096]{1,0:T(2,128)(2,1)S(1)} %copy-done, bf16[2,2,512]{2,1,0:T(2,128)(2,1)S(1)} %copy-done.1, ...), custom_call_target="tpu_custom_call" | custom-call | tf_op jit(solution)/shard_map/attend/pallas_call | solution.py:413
  20.4 12.0 %all_to_all.15.parts_ref = s16[16,72,128]{2,1,0:T(8,128)(2,1)S(1)} all-to-all(s16[16,72,128]{2,1,0:T(8,128)(2,1)S(1)} %get-tuple-element.11), channel_id=1, replica_groups=mesh['inst'=16,'page'=8,'head'=2] {'inst'}, dimensions={0} | all-to-all | bytes 589824 | tf_op jit(solution)/shard_map/all_to_all | solution.py:430
  32.5 0.5 combine.1
  32.9 17.5 %all_to_all.16.parts_ref = s16[8,72,128]{2,1,0:T(8,128)(2,1)S(1)} all-to-all(s16[8,72,128]{2,1,0:T(8,128)(2,1)S(1)} %combine.1), channel_id=1, replica_groups=mesh['inst'=16,'page'=8,'head'=2] {'page'}, dimensions={0} | all-to-all | bytes 294912 | tf_op jit(solution)/shard_map/all_to_all | solution.py:440
  50.5 0.9 %finish.1 = bf16[2,4096]{1,0:T(2,128)(2,1)} custom-call(s16[8,72,128]{2,1,0:T(8,128)(2,1)S(1)} %all_to_all.16.parts_ref, f32[16,128]{1,0:T(8,128)S(1)} %get-tuple-element.12.token_ref), custom_call_target="tpu_custom_call" | custom-call | tf_op jit(solution)/shard_map/finish/pallas_call | solution.py:442
Async XLA Ops:
  1.7 14.8 %all-to-all-start = ((bf16[16,72,128]{2,1,0:T(8,128)(2,1)}), bf16[16,72,128]{2,1,0:T(8,128)(2,1)S(1)}, u32[]{:S(2)}, u32[]{:S(2)}) async-start(bf16[16,72,128]{2,1,0:T(8,128)(2,1)} %send.1), calls=%async_computation | async-start | bytes 589824 | tf_op jit(solution)/shard_map/all_to_all | solution.py:392
  9.1 7.4 %copy-start = (bf16[2,4096]{1,0:T(2,128)(2,1)S(1)}, bf16[2,4096]{1,0:T(2,128)(2,1)}, u32[]{:S(2)}) copy-start(bf16[2,4096]{1,0:T(2,128)(2,1)} %queries_ref.3) | copy-start | bytes 49156
  9.1 7.4 %copy-start.1 = (bf16[2,2,512]{2,1,0:T(2,128)(2,1)S(1)}, bf16[2,2,512]{2,1,0:T(2,128)(2,1)}, u32[]{:S(2)}) copy-start(bf16[2,2,512]{2,1,0:T(2,128)(2,1)} %fresh_ref.1) | copy-start | bytes 12292
